TPU v7x, 128 devices: a whole 4x4x4 slice. The times are simulated.
128 devices in a mesh: node: 16 (over x, y), local: 8 (over z, core).
Axes of the slice: x: 4, y: 4, z: 4, core: 2. Of those that a mesh axis runs over, the one named last changes fastest.
Arguments:
- tokens: bfloat16 [16384, 4096], P(('node', 'local')), may hold values from -6 to 6
- routes: int32 [16384, 8], P(('node', 'local')), may hold values from 0 to 127, all different within a row; in each aligned block of 128 rows (0 to 127, 128 to 255, ...) at most 10 rows name the same one
- gates: float32 [16384, 8], P(('node', 'local')), may hold values from 0.05 to 1
- placement: int32 [128], replicated, may hold values from 0 to 127, each once
- w_gate: bfloat16 [128, 4096, 768], P(('node', 'local')), may hold values from -0.09375 to 0.09375
- w_up: bfloat16 [128, 4096, 768], P(('node', 'local')), may hold values from -0.09375 to 0.09375
- w_down: bfloat16 [128, 768, 4096], P(('node', 'local')), may hold values from -0.21875 to 0.21875
Outputs:
- mixed: bfloat16 [16384, 4096], P(('node', 'local'))
Inputs may be any that keep to these rules, and one draw needn't show every extreme that they name: `routes`: in each block of 128 rows no expert is named more than 10 times, some expert exactly 10 times; a row never names an expert twice. `placement`: every slot holds exactly one expert.
All inputs are finite; a program needn't handle non-finite values.
Results may differ from a plain program's by a relative error of at most 0.008.
Values may be sent and summed in bfloat16 or wider, within the bound.
No kernel may reach another device: no remote copies, remote signals or barrier semaphores. Data moves between devices by JAX's collectives and lax.ppermute only.
A program may use at most 128 MiB of HBM per device.

v0:
```python
import jax
import jax.numpy as jnp
from jax import lax
from jax.sharding import PartitionSpec as P


def expert_ffn(rows, w_gate, w_up, w_down):
    shape = rows.shape
    flat = rows.reshape(-1, shape[-1])
    gate = jnp.dot(flat, w_gate[0], preferred_element_type=jnp.float32)
    up = jnp.dot(flat, w_up[0], preferred_element_type=jnp.float32)
    hidden = (jax.nn.silu(gate) * up).astype(jnp.bfloat16)
    result = jnp.dot(hidden, w_down[0], preferred_element_type=jnp.float32).astype(jnp.bfloat16)
    return result.reshape(shape)


def on_device(tokens, routes, gates, placement, w_gate, w_up, w_down):
    tok_rows = tokens.shape[0]
    width = tokens.shape[1]
    top = routes.shape[1]
    experts_all = placement.shape[0]
    capacity = max(2, tok_rows * top * 5 // (4 * experts_all))
    pairs = tok_rows * top
    flat_e = routes.reshape(-1)
    onehot = (flat_e[:, None] == jnp.arange(experts_all, dtype=jnp.int32)[None, :]).astype(
        jnp.int32
    )
    rank = jnp.sum(jnp.cumsum(onehot, axis=0) * onehot, axis=1) - 1
    home = jnp.sum(onehot * placement[None, :], axis=1)
    dest = home * capacity + rank
    slot_token = (
        jnp.full((experts_all * capacity,), -1, jnp.int32)
        .at[dest]
        .set(jnp.arange(pairs, dtype=jnp.int32) // top)
    )
    valid = slot_token >= 0
    send = jnp.where(
        valid[:, None], tokens[jnp.maximum(slot_token, 0)], jnp.zeros((), jnp.bfloat16)
    )
    send = send.reshape(experts_all, capacity, width)
    outputs = expert_ffn(
        lax.all_to_all(send, ("node", "local"), split_axis=0, concat_axis=0, tiled=True),
        w_gate,
        w_up,
        w_down,
    )
    back = lax.all_to_all(outputs, ("node", "local"), split_axis=0, concat_axis=0, tiled=True)
    returned = back.reshape(-1, width)[dest].reshape(tok_rows, top, width)
    mixed = jnp.einsum("tkd,tk->td", returned.astype(jnp.float32), gates)
    return mixed.astype(jnp.bfloat16)


def solution(mesh):
    placed = (
        P(("node", "local"), None),
        P(("node", "local"), None),
        P(("node", "local"), None),
        P(),
        P(("node", "local"), None, None),
        P(("node", "local"), None, None),
        P(("node", "local"), None, None),
    )
    return jax.shard_map(
        on_device, mesh=mesh, in_specs=placed, out_specs=P(("node", "local"), None), check_vma=False
    )
```

profile of v0, /device:TPU:103, one launch (start us, length us, event | category | flops | bytes accessed | tf_op | source)
XLA Modules:
  0.0 603.9 jit_solution(6100979454515591013)
XLA Ops:
  0.0 0.9 copy.8
  0.9 0.1 eq.29
  1.1 0.1 copy.10
  1.2 0.2 fusion.14
  1.5 0.1 copy.11
  1.6 1.2 select_reduce_fusion
  2.8 4.3 scatter_custom_fusion
  7.1 8.4 %gather_fusion = bf16[1280,4096]{1,0:T(8,128)(2,1)} fusion(bf16[128,4096]{1,0:T(8,128)(2,1)S(1)} %copy-done, s32[2048]{0:T(1024)S(1)} %pad_clamp_fusion), kind=kCustom, calls=%fused_computation | custom fusion | bytes 20976640 | tf_op jit(solution)/shard_map/gather | solution.py:38
  15.5 15.2 %gather.9 = bf16[128,10,4096]{2,1,0:T(8,128)(2,1)} reshape(bf16[1280,4096]{1,0:T(8,128)(2,1)} %gather_fusion) | data formatting | bytes 20971520 | tf_op jit(solution)/shard_map/gather | solution.py:38
  30.7 0.2 broadcast_in_dim.26
  30.8 8.3 %broadcast_select_fusion = bf16[128,10,4096]{2,1,0:T(8,128)(2,1)S(1)} fusion(bf16[128,10,4096]{2,1,0:T(8,128)(2,1)} %gather.9, pred[128,10]{1,0:T(8,128)(4,1)S(1)} %broadcast_in_dim.26), kind=kLoop, calls=%fused_computation.3 | loop fusion | flops 5242880 | bytes 20972800 | tf_op jit(solution)/shard_map/jit(_where)/select_n | solution.py:37
  39.1 199.2 %all_to_all.10 = bf16[128,10,4096]{2,1,0:T(8,128)(2,1)} all-to-all(bf16[128,10,4096]{2,1,0:T(8,128)(2,1)S(1)} %broadcast_select_fusion), channel_id=1, replica_groups=mesh['node'=16,'local'=8] {'node','local'}, dimensions={0} | all-to-all | bytes 20971520 | tf_op jit(solution)/shard_map/all_to_all | solution.py:42
  238.3 16.5 %reshape.70 = bf16[1280,4096]{1,0:T(8,128)(2,1)} reshape(bf16[128,10,4096]{2,1,0:T(8,128)(2,1)} %all_to_all.10) | data formatting | bytes 20971520 | tf_op jit(solution)/shard_map/reshape | solution.py:9
  254.8 12.3 %fusion.5 = f32[1280,768]{1,0:T(8,128)S(1)} fusion(bf16[1280,4096]{1,0:T(8,128)(2,1)} %reshape.70, bf16[1,4096,768]{2,1,0:T(8,128)(2,1)} %param.11), kind=kOutput, calls=%fused_computation.10 | convolution fusion | flops 8053063680 | bytes 20709376 | tf_op jit(solution)/shard_map/dot_general | solution.py:10
  267.1 11.2 %fusion.10 = bf16[1280,768]{1,0:T(8,128)(2,1)S(1)} fusion(bf16[1280,4096]{1,0:T(8,128)(2,1)S(1)} %copy-done.2, bf16[1,4096,768]{2,1,0:T(8,128)(2,1)} %param.12, f32[1280,768]{1,0:T(8,128)S(1)} %fusion.5), kind=kOutput, calls=%fused_computation.13 | convolution fusion | flops 8058961920 | bytes 22675456 | tf_op jit(solution)/shard_map/dot_general | solution.py:11
  278.3 13.5 %convolution_convert_fusion = bf16[1280,4096]{1,0:T(8,128)(2,1)} fusion(bf16[1280,768]{1,0:T(8,128)(2,1)S(1)} %fusion.10, bf16[1,768,4096]{2,1,0:T(8,128)(2,1)} %param.13), kind=kOutput, calls=%fused_computation.4 | convolution fusion | flops 8058306560 | bytes 18743296 | tf_op jit(solution)/shard_map/dot_general | solution.py:13
  291.9 15.2 %reshape.71 = bf16[128,10,4096]{2,1,0:T(8,128)(2,1)} reshape(bf16[1280,4096]{1,0:T(8,128)(2,1)} %convolution_convert_fusion) | data formatting | bytes 20971520 | tf_op jit(solution)/shard_map/reshape | solution.py:14
  307.1 11.8 %all-to-all-start.1 = ((bf16[128,10,4096]{2,1,0:T(8,128)(2,1)}), bf16[128,10,4096]{2,1,0:T(8,128)(2,1)}, u32[]{:S(2)}, u32[]{:S(2)}) async-start(bf16[128,10,4096]{2,1,0:T(8,128)(2,1)} %reshape.71), calls=%async_computation.1 | async-start | bytes 33554432 | tf_op jit(solution)/shard_map/all_to_all | solution.py:47
  318.9 0.1 copy.12
  319.1 240.0 %all-to-all-done.1 = bf16[128,10,4096]{2,1,0:T(8,128)(2,1)} async-done(((bf16[128,10,4096]{2,1,0:T(8,128)(2,1)}), bf16[128,10,4096]{2,1,0:T(8,128)(2,1)}, u32[]{:S(2)}, u32[]{:S(2)}) %all-to-all-start.1) | async-done | bytes 10485792 | tf_op jit(solution)/shard_map/all_to_all | solution.py:47
  559.0 16.5 %reshape.72 = bf16[1280,4096]{1,0:T(8,128)(2,1)} reshape(bf16[128,10,4096]{2,1,0:T(8,128)(2,1)} %all-to-all-done.1) | data formatting | bytes 20971520 | tf_op jit(solution)/shard_map/reshape | solution.py:48
  575.6 20.5 %gather_fusion.1 = bf16[1024,4096]{1,0:T(8,128)(2,1)} fusion(bf16[1280,4096]{1,0:T(8,128)(2,1)} %reshape.72, s32[1024]{0:T(1024)S(1)} %broadcast_clamp_fusion), kind=kCustom, calls=%fused_computation.1 | custom fusion | bytes 16781312 | tf_op jit(solution)/shard_map/gather | solution.py:48
  596.1 5.7 fusion
  601.7 2.1 copy.15
  (20 shorter events, 0.2 us)
Async XLA Ops:
  0.0 7.1 %copy-start = (bf16[128,4096]{1,0:T(8,128)(2,1)S(1)}, bf16[128,4096]{1,0:T(8,128)(2,1)}, u32[]{:S(2)}) copy-start(bf16[128,4096]{1,0:T(8,128)(2,1)} %param.7) | copy-start | bytes 3145732
  254.8 12.3 %copy-start.2 = (bf16[1280,4096]{1,0:T(8,128)(2,1)S(1)}, bf16[1280,4096]{1,0:T(8,128)(2,1)}, u32[]{:S(2)}) copy-start(bf16[1280,4096]{1,0:T(8,128)(2,1)} %reshape.70) | copy-start | bytes 31457284
  307.0 11.9 %copy-start.3 = (f32[128,8]{0,1:T(8,128)S(1)}, f32[128,8]{0,1:T(8,128)}, u32[]{:S(2)}) copy-start(f32[128,8]{0,1:T(8,128)} %param.9) | copy-start | bytes 12292
  307.1 252.0 %all-to-all-start.1 = ((bf16[128,10,4096]{2,1,0:T(8,128)(2,1)}), bf16[128,10,4096]{2,1,0:T(8,128)(2,1)}, u32[]{:S(2)}, u32[]{:S(2)}) async-start(bf16[128,10,4096]{2,1,0:T(8,128)(2,1)} %reshape.71), calls=%async_computation.1 | async-start | bytes 33554432 | tf_op jit(solution)/shard_map/all_to_all | solution.py:47
  575.6 28.3 %copy-start.1 = (bf16[128,4096]{1,0:T(8,128)(2,1)S(1)}, bf16[128,4096]{1,0:T(8,128)(2,1)}, u32[]{:S(2)}) copy-start(bf16[128,4096]{1,0:T(8,128)(2,1)} %param.7) | copy-start | bytes 3145732
where the time goes:
time: 606 us; the launch traced here: 604 us
  waiting for transfers between devices  240 us (40%)
  blocking collectives  199 us (33%)
  local copies, waits for them, and re-layouts  100 us (17%)
  matrix products  42.7 us (7%)
  starting transfers between devices  11.8 us (2%)
  other arithmetic  9.74 us (2%)
    all_to_all x1, waiting for transfers between devices, on_device(): lax.all_to_all(outputs, ('node', 'local'), split_axis=0, concat_axis=0, t...  240 us
    all_to_all x1, blocking collectives, on_device(): lax.all_to_all(send, ('node', 'local'), split_axis=0, concat_axis=0, tile...  199 us
    gather x2, local copies, waits for them, and re-layouts, on_device(): tokens[jnp.maximum(slot_token, 0)]  23.6 us
    gather x1, local copies, waits for them, and re-layouts, on_device(): returned = back.reshape(-1, width)[dest].reshape(tok_rows, top, width)  20.5 us
    reshape x1, local copies, waits for them, and re-layouts, expert_ffn(): flat = rows.reshape(-1, shape[-1])  16.5 us
    reshape x1, local copies, waits for them, and re-layouts, on_device(): returned = back.reshape(-1, width)[dest].reshape(tok_rows, top, width)  16.5 us
    reshape x1, local copies, waits for them, and re-layouts, expert_ffn(): return result.reshape(shape)  15.2 us
    dot_general x1, matrix products, expert_ffn(): jnp.dot(hidden, w_down[0], preferred_element_type=jnp.float32)  13.5 us
  transfers between devices with their start and end apart: 1, of which 1 were waited for; matrix products, arithmetic and copies ran while one was open for 0% of the time, Pallas kernels for 0%

commit v1 on v0

v1 whole, which is shorter than its diff:
```python
import functools

import jax
import jax.numpy as jnp
from jax import lax
from jax.experimental import pallas as pl
from jax.experimental.pallas import tpu as pltpu
from jax.sharding import PartitionSpec as P

AXES = ("node", "local")
F32 = jnp.float32
BF16 = jnp.bfloat16
VMEM_BYTES = 60 << 20


def iota(shape, dim):
    return lax.broadcasted_iota(jnp.int32, shape, dim)


def dot(a, b):
    return jnp.dot(a, b, preferred_element_type=F32)


def rank_by_slot(routes_t, place_row):
    top, tok = routes_t.shape
    slots = place_row.shape[1]
    rows = iota((slots, tok), 0)
    chosen = jnp.zeros((slots, tok), F32)
    for k in range(top):
        chosen = chosen + (routes_t[k : k + 1, :] == rows).astype(F32)
    perm = (place_row == iota((slots, slots), 0)).astype(F32).astype(BF16)
    at_slot = dot(perm, chosen.astype(BF16))
    before = (iota((tok, tok), 0) < iota((tok, tok), 1)).astype(F32).astype(BF16)
    rank = dot(at_slot.astype(BF16), before)
    return jnp.where(at_slot > 0.5, rank, -1.0)


def pack_main_kernel(routes_ref, place_ref, tok_ref, out_ref, key_ref, sel_ref):
    slots, tok = key_ref.shape

    @pl.when(pl.program_id(0) == 0)
    def _():
        key = rank_by_slot(routes_ref[...], place_ref[...])
        key_ref[...] = key
        hit = key[:, None, :] == iota((slots, 8, tok), 1).astype(F32)
        sel_ref[...] = hit.astype(F32).reshape(slots * 8, tok).astype(BF16)

    out_ref[...] = dot(sel_ref[...], tok_ref[...]).astype(BF16)


def pack_over_kernel(key_ref, tok_ref, out_ref):
    slots, tok = key_ref.shape
    wide = out_ref.shape[1]
    key = jnp.broadcast_to(key_ref[...][:, None, :], (slots, 8, tok))
    j = iota((slots, 8, tok), 1)
    hit = key == (8 + j % 2).astype(F32)
    total = None
    for q in range(4):
        sel = (hit & (j // 2 == q)).astype(F32).reshape(slots * 8, tok).astype(BF16)
        part = dot(sel, tok_ref[:, q * wide : (q + 1) * wide])
        total = part if total is None else total + part
    out_ref[...] = total.astype(BF16)


def silu_mul(gate, up):
    return (gate / (1.0 + jnp.exp(-gate)) * up).astype(BF16)


def ffn_main_kernel(x_ref, wg_ref, wu_ref, wd_ref, out_ref, gate_ref, up_ref, hid_ref):
    step = pl.program_id(0)
    rows = x_ref.shape[0]
    block = 256

    def project(first):
        for m in range(0, rows, block):
            ms = slice(m, m + block)
            x = x_ref[ms, :]
            gate = dot(x, wg_ref[0])
            up = dot(x, wu_ref[0])
            if not first:
                gate = gate + gate_ref[ms, :]
                up = up + up_ref[ms, :]
            gate_ref[ms, :] = gate
            up_ref[ms, :] = up

    @pl.when(step == 0)
    def _():
        project(True)

    @pl.when((step > 0) & (step < 4))
    def _():
        project(False)

    @pl.when(step == 4)
    def _():
        for m in range(0, rows, block):
            ms = slice(m, m + block)
            hid_ref[ms, :] = silu_mul(gate_ref[ms, :], up_ref[ms, :])

    @pl.when(step >= 4)
    def _():
        for m in range(0, rows, block):
            out = dot(hid_ref[m : m + block, :], wd_ref[0])
            out_ref[m // 8 : (m + block) // 8] = out.reshape(block // 8, 8, out.shape[1]).astype(BF16)


def ffn_over_kernel(buf_ref, x_ref, wg_ref, wu_ref, wd_ref, out_ref, wide_ref, gate_ref, up_ref, hid_ref):
    del buf_ref
    step = pl.program_id(0)
    slots = out_ref.shape[0]
    width = out_ref.shape[2]

    @pl.when(step == 0)
    def _():
        for c in range(width // 128):
            wide_ref[c] = x_ref[:, c * 128 : (c + 1) * 128].astype(F32)
        gate_ref[...] = jnp.zeros_like(gate_ref)
        up_ref[...] = jnp.zeros_like(up_ref)

    for q in range(4):

        @pl.when(step == q)
        def _(q=q):
            x = jnp.concatenate(
                [
                    jnp.concatenate(
                        [wide_ref[c, pl.ds(2 * q + r, slots, stride=8), :].astype(BF16) for c in range(width // 128)],
                        axis=1,
                    )
                    for r in range(2)
                ],
                axis=0,
            )
            gate_ref[...] += dot(x, wg_ref[0])
            up_ref[...] += dot(x, wu_ref[0])

    @pl.when(step == 4)
    def _():
        hid_ref[...] = silu_mul(gate_ref[...], up_ref[...])

    for q in range(4):

        @pl.when(step == 4 + q)
        def _(q=q):
            out = dot(hid_ref[...], wd_ref[0])
            for r in range(2):
                for c in range(width // 128):
                    wide_ref[c, pl.ds(2 * q + r, slots, stride=8), :] = out[
                        r * slots : (r + 1) * slots, c * 128 : (c + 1) * 128
                    ]

    @pl.when(step == 7)
    def _():
        for c in range(width // 128):
            out_ref[:, :, c * 128 : (c + 1) * 128] = wide_ref[c].reshape(slots, 8, 128).astype(BF16)


def combine_kernel(routes_ref, gates_ref, place_ref, main_ref, over_ref, out_ref, cmain_ref, cover_ref):
    tok, top = routes_ref.shape
    slots = place_ref.shape[0]
    q = pl.program_id(0)

    @pl.when((q == 0) & (pl.program_id(1) == 0))
    def _():
        lanes = iota((tok, slots), 1)
        chosen = jnp.zeros((tok, slots), F32)
        weight = jnp.zeros((tok, slots), F32)
        for k in range(top):
            hit = (routes_ref[:, k : k + 1] == lanes).astype(F32)
            chosen = chosen + hit
            weight = weight + hit * gates_ref[:, k : k + 1]
        perm = (place_ref[...] == iota((slots, slots), 1)).astype(F32).astype(BF16)
        high = weight.astype(BF16)
        low = (weight - high.astype(F32)).astype(BF16)
        at_slot = dot(chosen.astype(BF16), perm)
        before = (iota((tok, tok), 1) < iota((tok, tok), 0)).astype(F32).astype(BF16)
        rank = dot(before, at_slot.astype(BF16))
        key = jnp.where(at_slot > 0.5, rank, -1.0).astype(BF16)
        spread = (iota((slots, slots * 8), 1) // 8 == iota((slots, slots * 8), 0)).astype(F32).astype(BF16)
        key = dot(key, spread)
        high = dot(dot(high, perm).astype(BF16), spread)
        low = dot(dot(low, perm).astype(BF16), spread)
        j = iota((tok, slots * 8), 1) % 8
        hit = key == j.astype(F32)
        cmain_ref[:tok, :] = jnp.where(hit, high, 0.0).astype(BF16)
        cmain_ref[tok:, :] = jnp.where(hit, low, 0.0).astype(BF16)
        hit = key == (8 + j % 2).astype(F32)
        for p in range(4):
            here = hit & (j // 2 == p)
            cover_ref[p, :tok, :] = jnp.where(here, high, 0.0).astype(BF16)
            cover_ref[p, tok:, :] = jnp.where(here, low, 0.0).astype(BF16)

    rows = slots * 8
    wide = out_ref.shape[1]
    total = dot(cmain_ref[...], main_ref[...].reshape(rows, wide))
    total = total + dot(cover_ref[q], over_ref[...].reshape(rows, wide))
    out_ref[...] = (total[:tok] + total[tok:]).astype(BF16)


def params(grid_dims):
    return pltpu.CompilerParams(dimension_semantics=("arbitrary",) * grid_dims, vmem_limit_bytes=VMEM_BYTES)


def shape(dims, kind=BF16):
    return jax.ShapeDtypeStruct(dims, kind)


def on_device(tokens, routes, gates, placement, w_gate, w_up, w_down):
    tok, width = tokens.shape
    slots = placement.shape[0]
    hid = w_gate.shape[2]
    rows = slots * 8
    wide = width // 4
    exchange = functools.partial(lax.all_to_all, axis_name=AXES, split_axis=0, concat_axis=0, tiled=True)
    whole = lambda *dims: pl.BlockSpec(dims, lambda *_: (0,) * len(dims))

    main, key = pl.pallas_call(
        pack_main_kernel,
        name="pack_main",
        grid=(4,),
        in_specs=[whole(routes.shape[1], tok), whole(1, slots), pl.BlockSpec((tok, wide), lambda i: (0, i))],
        out_specs=[pl.BlockSpec((rows, wide), lambda i: (0, i)), whole(slots, tok)],
        out_shape=[shape((rows, width)), shape((slots, tok), F32)],
        scratch_shapes=[pltpu.VMEM((rows, tok), BF16)],
        compiler_params=params(1),
    )(routes.T, placement.reshape(1, slots), tokens)
    over = pl.pallas_call(
        pack_over_kernel,
        name="pack_over",
        grid=(1,),
        in_specs=[whole(slots, tok), whole(tok, width)],
        out_specs=whole(rows, wide),
        out_shape=shape((rows, wide)),
        compiler_params=params(1),
    )(key, tokens)

    main = exchange(main.reshape(slots, 8, width)).reshape(rows, width)
    over = exchange(over.reshape(slots, 8, wide)).reshape(rows, wide)

    early = lambda i: jnp.minimum(i, 3)
    late = lambda i: jnp.maximum(i - 4, 0)
    weights = [
        pl.BlockSpec((1, wide, hid), lambda i: (0, early(i), 0)),
        pl.BlockSpec((1, wide, hid), lambda i: (0, early(i), 0)),
        pl.BlockSpec((1, hid, wide), lambda i: (0, 0, late(i))),
    ]
    buf = pl.pallas_call(
        ffn_main_kernel,
        name="ffn_main",
        grid=(8,),
        in_specs=[pl.BlockSpec((rows, wide), lambda i: (0, early(i)))] + weights,
        out_specs=pl.BlockSpec((slots, 8, wide), lambda i: (0, late(i), 0)),
        out_shape=shape((slots, 40, wide)),
        scratch_shapes=[pltpu.VMEM((rows, hid), F32), pltpu.VMEM((rows, hid), F32), pltpu.VMEM((rows, hid), BF16)],
        compiler_params=params(1),
    )(main, w_gate, w_up, w_down)
    buf = pl.pallas_call(
        ffn_over_kernel,
        name="ffn_over",
        grid=(8,),
        in_specs=[pl.BlockSpec(memory_space=pl.ANY), whole(rows, wide)] + weights,
        out_specs=pl.BlockSpec((slots, 8, wide), lambda i: (0, 4, 0)),
        out_shape=shape((slots, 40, wide)),
        scratch_shapes=[
            pltpu.VMEM((wide // 128, rows, 128), F32),
            pltpu.VMEM((2 * slots, hid), F32),
            pltpu.VMEM((2 * slots, hid), F32),
            pltpu.VMEM((2 * slots, hid), BF16),
        ],
        input_output_aliases={0: 0},
        compiler_params=params(1),
    )(buf, over, w_gate, w_up, w_down)
    back = exchange(buf)

    half = wide // 2
    return pl.pallas_call(
        combine_kernel,
        name="combine",
        grid=(4, 2),
        in_specs=[
            whole(tok, routes.shape[1]),
            whole(tok, routes.shape[1]),
            whole(slots, 1),
            pl.BlockSpec((slots, 8, half), lambda i, h: (0, i, h)),
            pl.BlockSpec((slots, 8, half), lambda i, h: (0, 4, h)),
        ],
        out_specs=pl.BlockSpec((tok, half), lambda i, h: (0, 2 * i + h)),
        out_shape=shape((tok, width)),
        scratch_shapes=[pltpu.VMEM((2 * tok, rows), BF16), pltpu.VMEM((4, 2 * tok, rows), BF16)],
        compiler_params=params(2),
    )(routes, gates, placement.reshape(slots, 1), back, back)


def solution(mesh):
    placed = (
        P(AXES, None),
        P(AXES, None),
        P(AXES, None),
        P(),
        P(AXES, None, None),
        P(AXES, None, None),
        P(AXES, None, None),
    )
    return jax.shard_map(on_device, mesh=mesh, in_specs=placed, out_specs=P(AXES, None), check_vma=False)
```

time: 606 us -> 329 us (0.54)
  blocking collectives: 199 us -> 0 us
  local copies, waits for them, and re-layouts: 100 us -> 3.53 us
  Pallas kernels: 0 us -> 66.2 us
  matrix products: 42.7 us -> 0 us
  starting transfers between devices: 11.8 us -> 27.4 us
  waiting for transfers between devices: 240 us -> 229 us
  other arithmetic: 9.74 us -> 0 us
    all_to_all x1 -> x0, blocking collectives: 199 us -> none  [on_device(): lax.all_to_all(send, ('node', 'local'), split_axis=0, concat_axis=0, tile...]
    pallas_call x0 -> x5, Pallas kernels: none -> 66.2 us  [the longest x1 26.9 us: on_device(): pl.pallas_call(ffn_main_kernel, name='ffn_main', grid=(8,), in_specs=[pl....]
    reshape x3 -> x1, local copies, waits for them, and re-layouts: 48.2 us -> 0.75 us  [on_device(): placement.reshape(slots, 1)]
    gather x3 -> x0, local copies, waits for them, and re-layouts: 44 us -> none  [the longest x2 23.6 us: on_device(): tokens[jnp.maximum(slot_token, 0)]]
    dot_general x4 -> x0, matrix products: 42.7 us -> none  [the longest x1 13.5 us: expert_ffn(): jnp.dot(hidden, w_down[0], preferred_element_type=jnp.float32)]
    all_to_all x1 -> x3, starting transfers between devices: 11.8 us -> 27.4 us  [the longest x1 10.6 us: on_device(): main = exchange(main.reshape(slots, 8, width)).reshape(rows, width)]
    all_to_all x1 -> x3, waiting for transfers between devices: 240 us -> 229 us  [the longest x1 130 us: on_device(): back = exchange(buf)]
    select_n x3 -> x0, other arithmetic: 8.29 us -> none  [the longest x1 8.28 us: on_device(): jnp.where(valid[:, None], tokens[jnp.maximum(slot_token, 0)], jnp.zeros((...]
  transfers between devices with their start and end apart: 1 -> 3, of which waited for: 1 -> 2; matrix products, arithmetic and copies ran while one was open for 0% -> 1% of each run, Pallas kernels for 0% -> 10%
where the time goes in v1:
time: 329 us; the launch traced here: 326 us
  waiting for transfers between devices  229 us (70%)
  Pallas kernels  66.2 us (20%)
  starting transfers between devices  27.4 us (8%)
  local copies, waits for them, and re-layouts  3.53 us (1%)
    all_to_all x1, waiting for transfers between devices, on_device(): back = exchange(buf)  130 us
    all_to_all x1, waiting for transfers between devices, on_device(): main = exchange(main.reshape(slots, 8, width)).reshape(rows, width)  98.7 us
    pallas_call x1, Pallas kernels, on_device(): pl.pallas_call(ffn_main_kernel, name='ffn_main', grid=(8,), in_specs=[pl....  26.9 us
    pallas_call x1, Pallas kernels, on_device(): pl.pallas_call(ffn_over_kernel, name='ffn_over', grid=(8,), in_specs=[pl....  15.1 us
    pallas_call x1, Pallas kernels, on_device(): pl.pallas_call(combine_kernel, name='combine', grid=(4, 2), in_specs=[who...  12.7 us
    all_to_all x1, starting transfers between devices, on_device(): main = exchange(main.reshape(slots, 8, width)).reshape(rows, width)  10.6 us
    all_to_all x1, starting transfers between devices, on_device(): back = exchange(buf)  10.2 us
    all_to_all x1, starting transfers between devices, on_device(): over = exchange(over.reshape(slots, 8, wide)).reshape(rows, wide)  6.69 us
  transfers between devices with their start and end apart: 3, of which 2 were waited for; matrix products, arithmetic and copies ran while one was open for 1% of the time, Pallas kernels for 10%

profile of v1, /device:TPU:103, one launch (start us, length us, event | category | flops | bytes accessed | tf_op | source)
XLA Modules:
  0.0 325.8 jit_solution(8904413676824066964)
XLA Ops:
  0.0 6.5 %pack_main.1 = (bf16[1024,4096]{1,0:T(8,128)(2,1)}, f32[128,128]{1,0:T(8,128)}) custom-call(s32[8,128]{1,0:T(8,128)} %bitcast.10, s32[1,128]{1,0:T(1,128)} %bitcast.11, bf16[128,4096]{1,0:T(8,128)(2,1)} %tok_ref.3), custom_call_target="tpu_custom_call" | custom-call | tf_op jit(solution)/shard_map/pack_main/pallas_call | solution.py:217
  6.5 10.6 %all-to-all-start = ((bf16[128,8,4096]{2,1,0:T(8,128)(2,1)}), bf16[128,8,4096]{2,1,0:T(8,128)(2,1)}, u32[]{:S(2)}, u32[]{:S(2)}) async-start(bf16[128,8,4096]{2,1,0:T(8,128)(2,1)} %bitcast.8), calls=%async_computation | async-start | bytes 16777216 | tf_op jit(solution)/shard_map/all_to_all | solution.py:237
  17.1 4.9 %pack_over.1 = bf16[1024,1024]{1,0:T(8,128)(2,1)} custom-call(f32[128,128]{1,0:T(8,128)} %get-tuple-element.8.key_ref, bf16[128,4096]{1,0:T(8,128)(2,1)} %tok_ref.3), custom_call_target="tpu_custom_call" | custom-call | tf_op jit(solution)/shard_map/pack_over/pallas_call | solution.py:227
  22.0 98.7 %all-to-all-done = bf16[128,8,4096]{2,1,0:T(8,128)(2,1)} async-done(((bf16[128,8,4096]{2,1,0:T(8,128)(2,1)}), bf16[128,8,4096]{2,1,0:T(8,128)(2,1)}, u32[]{:S(2)}, u32[]{:S(2)}) %all-to-all-start) | async-done | bytes 8388640 | tf_op jit(solution)/shard_map/all_to_all | solution.py:237
  120.7 6.7 %all-to-all-start.1 = ((bf16[128,8,1024]{2,1,0:T(8,128)(2,1)}), bf16[128,8,1024]{2,1,0:T(8,128)(2,1)S(1)}, u32[]{:S(2)}, u32[]{:S(2)}) async-start(bf16[128,8,1024]{2,1,0:T(8,128)(2,1)} %bitcast.9), calls=%async_computation.1 | async-start | bytes 4194304 | tf_op jit(solution)/shard_map/all_to_all | solution.py:238
  127.4 26.9 %ffn_main.1.buf_ref = bf16[128,40,1024]{2,1,0:T(8,128)(2,1)} custom-call(bf16[1024,4096]{1,0:T(8,128)(2,1)} %bitcast.4.x_ref, bf16[1,4096,768]{2,1,0:T(8,128)(2,1)} %wg_ref.3, bf16[1,4096,768]{2,1,0:T(8,128)(2,1)} %wu_ref.3, bf16[1,768,4096]{2,1,0:T(8,128)(2,1)} %wd_ref.3), custom_call_target="tpu_custom_call" | custom-call | tf_op jit(solution)/shard_map/ffn_main/pallas_call | solution.py:247
  154.3 0.0 all-to-all-done.1
  154.3 0.0 copy-start
  154.3 1.3 copy-done
  155.6 15.1 %ffn_over.1 = bf16[128,40,1024]{2,1,0:T(8,128)(2,1)} custom-call(bf16[128,40,1024]{2,1,0:T(8,128)(2,1)} %ffn_main.1.buf_ref, bf16[1024,1024]{1,0:T(8,128)(2,1)} %bitcast.7, bf16[1,4096,768]{2,1,0:T(8,128)(2,1)} %wg_ref.3, bf16[1,4096,768]{2,1,0:T(8,128)(2,1)} %wu_ref.3, bf16[1,768,4096]{2,1,0:T(8,128)(2,1)} %wd_ref.3), custom_call_target="tpu_custom_call", output_to_operand_aliasing={{}: (0, {})} | custom-call | tf_op jit(solution)/shard_map/ffn_over/pallas_call | solution.py:257
  170.8 0.0 copy-start.1
  170.8 0.0 copy-start.2
  170.8 0.0 copy-start.3
  170.8 10.2 %all-to-all-start.2 = ((bf16[128,40,1024]{2,1,0:T(8,128)(2,1)}), bf16[128,40,1024]{2,1,0:T(8,128)(2,1)}, u32[]{:S(2)}, u32[]{:S(2)}) async-start(bf16[128,40,1024]{2,1,0:T(8,128)(2,1)} %ffn_over.1), calls=%async_computation.2 | async-start | bytes 20971520 | tf_op jit(solution)/shard_map/all_to_all | solution.py:273
  180.9 0.0 copy-done.1
  181.0 0.7 copy.9.routes_ref
  181.7 0.0 copy-done.2
  181.7 0.7 copy.10.gates_ref
  182.4 0.0 copy-done.3
  182.4 0.7 copy.11.place_ref
  183.1 129.9 %all-to-all-done.2.main_ref.over_ref = bf16[128,40,1024]{2,1,0:T(8,128)(2,1)} async-done(((bf16[128,40,1024]{2,1,0:T(8,128)(2,1)}), bf16[128,40,1024]{2,1,0:T(8,128)(2,1)}, u32[]{:S(2)}, u32[]{:S(2)}) %all-to-all-start.2) | async-done | bytes 10485792 | tf_op jit(solution)/shard_map/all_to_all | solution.py:273
  313.0 12.7 %combine.1 = bf16[128,4096]{1,0:T(8,128)(2,1)} custom-call(s32[128,8]{1,0:T(8,128)} %copy.9.routes_ref, f32[128,8]{1,0:T(8,128)} %copy.10.gates_ref, s32[128,1]{1,0:T(8,128)} %copy.11.place_ref, bf16[128,40,1024]{2,1,0:T(8,128)(2,1)} %all-to-all-done.2.main_ref.over_ref, bf16[128,40,1024]{2,1,0:T(8,128)(2,1)} %all-to-all-done.2.main_ref.over_ref), custom_call_target="tpu_custom_call" | custom-call | tf_op jit(solution)/shard_map/combine/pallas_call | solution.py:276
Async XLA Ops:
  6.5 114.2 %all-to-all-start = ((bf16[128,8,4096]{2,1,0:T(8,128)(2,1)}), bf16[128,8,4096]{2,1,0:T(8,128)(2,1)}, u32[]{:S(2)}, u32[]{:S(2)}) async-start(bf16[128,8,4096]{2,1,0:T(8,128)(2,1)} %bitcast.8), calls=%async_computation | async-start | bytes 16777216 | tf_op jit(solution)/shard_map/all_to_all | solution.py:237
  120.7 33.6 %all-to-all-start.1 = ((bf16[128,8,1024]{2,1,0:T(8,128)(2,1)}), bf16[128,8,1024]{2,1,0:T(8,128)(2,1)S(1)}, u32[]{:S(2)}, u32[]{:S(2)}) async-start(bf16[128,8,1024]{2,1,0:T(8,128)(2,1)} %bitcast.9), calls=%async_computation.1 | async-start | bytes 4194304 | tf_op jit(solution)/shard_map/all_to_all | solution.py:238
  154.3 1.3 copy-start
  170.8 10.2 %copy-start.1 = (s32[128,8]{0,1:T(8,128)S(1)}, s32[128,8]{0,1:T(8,128)}, u32[]{:S(2)}) copy-start(s32[128,8]{0,1:T(8,128)} %param.8) | copy-start | bytes 12292
  170.8 10.9 %copy-start.2 = (f32[128,8]{0,1:T(8,128)S(1)}, f32[128,8]{0,1:T(8,128)}, u32[]{:S(2)}) copy-start(f32[128,8]{0,1:T(8,128)} %param.9) | copy-start | bytes 12292
  170.8 11.6 %copy-start.3 = (s32[128]{0:T(128)S(1)}, s32[128]{0:T(128)}, u32[]{:S(2)}) copy-start(s32[128]{0:T(128)} %param.10) | copy-start | bytes 1540
  170.8 142.3 %all-to-all-start.2 = ((bf16[128,40,1024]{2,1,0:T(8,128)(2,1)}), bf16[128,40,1024]{2,1,0:T(8,128)(2,1)}, u32[]{:S(2)}, u32[]{:S(2)}) async-start(bf16[128,40,1024]{2,1,0:T(8,128)(2,1)} %ffn_over.1), calls=%async_computation.2 | async-start | bytes 20971520 | tf_op jit(solution)/shard_map/all_to_all | solution.py:273

commit v2 on v1

v2 whole, which is shorter than its diff:
```python
import functools

import jax
import jax.numpy as jnp
from jax import lax
from jax.experimental import pallas as pl
from jax.experimental.pallas import tpu as pltpu
from jax.sharding import PartitionSpec as P

AXES = ("node", "local")
F32 = jnp.float32
BF16 = jnp.bfloat16


def iota(shape, dim):
    return lax.broadcasted_iota(jnp.int32, shape, dim)


def dot(a, b):
    return jnp.dot(a, b, preferred_element_type=F32)


def rank_by_slot(routes_t, place_row):
    top, tok = routes_t.shape
    slots = place_row.shape[1]
    rows = iota((slots, tok), 0)
    chosen = jnp.zeros((slots, tok), F32)
    for k in range(top):
        chosen = chosen + (routes_t[k : k + 1, :] == rows).astype(F32)
    perm = (place_row == iota((slots, slots), 0)).astype(F32).astype(BF16)
    at_slot = dot(perm, chosen.astype(BF16))
    before = (iota((tok, tok), 0) < iota((tok, tok), 1)).astype(F32).astype(BF16)
    rank = dot(at_slot.astype(BF16), before)
    return jnp.where(at_slot > 0.5, rank, -1.0)


GROUP = 32


def regroup(back):
    size = GROUP * 8
    grouped, plain = iota((size, size), 1 if back else 0), iota((size, size), 0 if back else 1)
    return (plain == grouped % GROUP * 8 + grouped // GROUP).astype(F32).astype(BF16)


def pack_kernel(routes_ref, place_ref, tok_ref, out_ref, key_ref, sel_ref, part_ref):
    step = pl.program_id(0)
    slots, tok = key_ref.shape
    groups = slots // GROUP
    wide = out_ref.shape[2]
    pair = GROUP * 2

    @pl.when(step == 0)
    def _():
        key = rank_by_slot(routes_ref[...], place_ref[...])
        key_ref[...] = key
        hit = key[:, None, :] == iota((slots, 8, tok), 1).astype(F32)
        sel_ref[...] = hit.astype(F32).reshape(slots * 8, tok).astype(BF16)

    for q in range(4):

        @pl.when(step == q)
        def _(q=q):
            out = dot(sel_ref[...], tok_ref[:, q * wide : (q + 1) * wide])
            out_ref[...] = out.reshape(slots, 8, wide).astype(BF16)

    @pl.when(step == 4)
    def _():
        sel = jnp.concatenate(
            [
                (key_ref[g * GROUP : (g + 1) * GROUP, :] == 8.0 + r).astype(F32)
                for g in range(groups)
                for r in range(2)
            ],
            axis=0,
        ).astype(BF16)
        for q in range(4):
            out = dot(sel, tok_ref[:, q * wide : (q + 1) * wide]).astype(BF16)
            for g in range(groups):
                part_ref[g, q * pair : (q + 1) * pair, :] = out[g * pair : (g + 1) * pair]
        order = regroup(True)
        for g in range(groups):
            out = dot(order, part_ref[g])
            out_ref[g * GROUP : (g + 1) * GROUP] = out.reshape(GROUP, 8, wide).astype(BF16)


def silu_mul(gate, up):
    return (gate / (1.0 + jnp.exp(-gate)) * up).astype(BF16)


def ffn_main_kernel(x_ref, wg_ref, wu_ref, wd_ref, out_ref, gate_ref, up_ref, hid_ref):
    step = pl.program_id(0)
    rows, wide = out_ref.shape
    block = 256

    def project(first):
        for m in range(0, rows, block):
            ms = slice(m, m + block)
            x = x_ref[m // 8 : (m + block) // 8].reshape(block, wide)
            gate = dot(x, wg_ref[0])
            up = dot(x, wu_ref[0])
            if not first:
                gate = gate + gate_ref[ms, :]
                up = up + up_ref[ms, :]
            gate_ref[ms, :] = gate
            up_ref[ms, :] = up

    @pl.when(step == 0)
    def _():
        project(True)

    @pl.when((step > 0) & (step < 4))
    def _():
        project(False)

    @pl.when(step == 4)
    def _():
        for m in range(0, rows, block):
            ms = slice(m, m + block)
            hid_ref[ms, :] = silu_mul(gate_ref[ms, :], up_ref[ms, :])

    @pl.when(step >= 4)
    def _():
        for m in range(0, rows, block):
            ms = slice(m, m + block)
            out_ref[ms, :] = dot(hid_ref[ms, :], wd_ref[0]).astype(BF16)


def ffn_over_kernel(x_ref, wg_ref, wu_ref, wd_ref, out_ref, part_ref, gate_ref, up_ref, hid_ref):
    step = pl.program_id(0)
    groups = part_ref.shape[0]
    wide = out_ref.shape[1]
    size = GROUP * 8
    pair = GROUP * 2

    @pl.when(step == 0)
    def _():
        order = regroup(False)
        for g in range(groups):
            x = x_ref[g * GROUP : (g + 1) * GROUP].reshape(size, wide)
            part_ref[g] = dot(order, x).astype(BF16)
        gate_ref[...] = jnp.zeros_like(gate_ref)
        up_ref[...] = jnp.zeros_like(up_ref)

    @pl.when(step < 4)
    def _():
        here = pl.ds(pl.multiple_of(step * pair, pair), pair)
        x = jnp.concatenate([part_ref[g, here, :] for g in range(groups)], axis=0)
        gate_ref[...] += dot(x, wg_ref[0])
        up_ref[...] += dot(x, wu_ref[0])

    @pl.when(step == 4)
    def _():
        hid_ref[...] = silu_mul(gate_ref[...], up_ref[...])

    @pl.when(step >= 4)
    def _():
        here = pl.ds(pl.multiple_of((step - 4) * pair, pair), pair)
        out = dot(hid_ref[...], wd_ref[0]).astype(BF16)
        for g in range(groups):
            part_ref[g, here, :] = out[g * pair : (g + 1) * pair]

    @pl.when(step == 7)
    def _():
        order = regroup(True)
        for g in range(groups):
            out_ref[g * size : (g + 1) * size, :] = dot(order, part_ref[g]).astype(BF16)


def weights_kernel(routes_ref, gates_ref, place_ref, cmain_ref, cover_ref):
    tok, top = routes_ref.shape
    slots = place_ref.shape[0]
    lanes = iota((tok, slots), 1)
    chosen = jnp.zeros((tok, slots), F32)
    weight = jnp.zeros((tok, slots), F32)
    for k in range(top):
        hit = (routes_ref[:, k : k + 1] == lanes).astype(F32)
        chosen = chosen + hit
        weight = weight + hit * gates_ref[:, k : k + 1]
    perm = (place_ref[...] == iota((slots, slots), 1)).astype(F32).astype(BF16)
    high = weight.astype(BF16)
    low = (weight - high.astype(F32)).astype(BF16)
    at_slot = dot(chosen.astype(BF16), perm)
    before = (iota((tok, tok), 1) < iota((tok, tok), 0)).astype(F32).astype(BF16)
    rank = dot(before, at_slot.astype(BF16))
    key = jnp.where(at_slot > 0.5, rank, -1.0).astype(BF16)
    high = dot(high, perm).astype(BF16)
    low = dot(low, perm).astype(BF16)

    def place(out_ref, slot_of, rank_of):
        width = out_ref.shape[1]
        lane = iota((slots, width), 1)
        spread = (slot_of(lane) == iota((slots, width), 0)).astype(F32).astype(BF16)
        hit = dot(key, spread) == rank_of(iota((tok, width), 1)).astype(F32)
        out_ref[:tok, :] = jnp.where(hit, dot(high, spread), 0.0).astype(BF16)
        out_ref[tok:, :] = jnp.where(hit, dot(low, spread), 0.0).astype(BF16)

    place(cmain_ref, lambda i: i // 8, lambda i: i % 8)
    place(cover_ref, lambda i: i // (2 * GROUP) * GROUP + i % GROUP, lambda i: 8 + i // GROUP % 2)


def combine_over_kernel(cover_ref, over_ref, out_ref):
    tok = out_ref.shape[0]
    wide = over_ref.shape[1]
    size = GROUP * 8
    pair = GROUP * 2
    order = regroup(False)
    parts = [
        dot(order, over_ref[i : i + size, :]).astype(BF16) for i in range(0, over_ref.shape[0], size)
    ]
    for q in range(4):
        over = jnp.concatenate([part[q * pair : (q + 1) * pair] for part in parts], axis=0)
        total = dot(cover_ref[...], over)
        out_ref[:, q * wide : (q + 1) * wide] = total[:tok] + total[tok:]


def combine_main_kernel(cmain_ref, main_ref, over_ref, out_ref):
    tok = out_ref.shape[0]
    total = dot(cmain_ref[...], main_ref[...])
    out_ref[...] = (total[:tok] + total[tok:] + over_ref[...]).astype(BF16)


def params(grid_dims, mib=60):
    return pltpu.CompilerParams(dimension_semantics=("arbitrary",) * grid_dims, vmem_limit_bytes=mib << 20)


def shape(dims, kind=BF16):
    return jax.ShapeDtypeStruct(dims, kind)


def on_device(tokens, routes, gates, placement, w_gate, w_up, w_down):
    tok, width = tokens.shape
    slots = placement.shape[0]
    hid = w_gate.shape[2]
    rows = slots * 8
    wide = width // 4
    exchange = functools.partial(lax.all_to_all, axis_name=AXES, split_axis=0, concat_axis=0, tiled=True)
    whole = lambda *dims: pl.BlockSpec(dims, lambda *_: (0,) * len(dims))

    sent = pl.pallas_call(
        pack_kernel,
        name="pack",
        grid=(5,),
        in_specs=[whole(routes.shape[1], tok), whole(1, slots), whole(tok, width)],
        out_specs=pl.BlockSpec((slots, 8, wide), lambda i: (0, i, 0)),
        out_shape=shape((slots, 40, wide)),
        scratch_shapes=[
            pltpu.VMEM((slots, tok), F32),
            pltpu.VMEM((rows, tok), BF16),
            pltpu.VMEM((slots // GROUP, 8 * GROUP, wide), BF16),
        ],
        compiler_params=params(1),
    )(routes.T, placement.reshape(1, slots), tokens)
    got = exchange(sent)
    cmain, cover = pl.pallas_call(
        weights_kernel,
        name="weights",
        grid=(1,),
        in_specs=[whole(tok, routes.shape[1]), whole(tok, routes.shape[1]), whole(slots, 1)],
        out_specs=[whole(2 * tok, rows), whole(2 * tok, 2 * slots)],
        out_shape=[shape((2 * tok, rows)), shape((2 * tok, 2 * slots))],
        compiler_params=params(1),
    )(routes, gates, placement.reshape(slots, 1))

    early = lambda i: jnp.minimum(i, 3)
    late = lambda i: jnp.maximum(i - 4, 0)
    weights = [
        pl.BlockSpec((1, wide, hid), lambda i: (0, early(i), 0)),
        pl.BlockSpec((1, wide, hid), lambda i: (0, early(i), 0)),
        pl.BlockSpec((1, hid, wide), lambda i: (0, 0, late(i))),
    ]
    over = pl.pallas_call(
        ffn_over_kernel,
        name="ffn_over",
        grid=(8,),
        in_specs=[pl.BlockSpec((slots, 8, wide), lambda i: (0, 4, 0))] + weights,
        out_specs=whole(rows, wide),
        out_shape=shape((rows, wide)),
        scratch_shapes=[
            pltpu.VMEM((slots // GROUP, 8 * GROUP, wide), BF16),
            pltpu.VMEM((2 * slots, hid), F32),
            pltpu.VMEM((2 * slots, hid), F32),
            pltpu.VMEM((2 * slots, hid), BF16),
        ],
        compiler_params=params(1),
    )(got, w_gate, w_up, w_down)
    over = exchange(over.reshape(slots, 8, wide)).reshape(rows, wide)
    main = pl.pallas_call(
        ffn_main_kernel,
        name="ffn_main",
        grid=(8,),
        in_specs=[pl.BlockSpec((slots, 8, wide), lambda i: (0, early(i), 0))] + weights,
        out_specs=pl.BlockSpec((rows, wide), lambda i: (0, late(i))),
        out_shape=shape((rows, width)),
        scratch_shapes=[pltpu.VMEM((rows, hid), F32), pltpu.VMEM((rows, hid), F32), pltpu.VMEM((rows, hid), BF16)],
        compiler_params=params(1),
    )(got, w_gate, w_up, w_down)
    main = exchange(main.reshape(slots, 8, width)).reshape(rows, width)

    total = pl.pallas_call(
        combine_over_kernel,
        name="combine_over",
        grid=(1,),
        in_specs=[whole(2 * tok, 2 * slots), whole(rows, wide)],
        out_specs=whole(tok, width),
        out_shape=shape((tok, width), F32),
        compiler_params=params(1),
    )(cover, over)
    half = wide // 2
    return pl.pallas_call(
        combine_main_kernel,
        name="combine_main",
        grid=(8,),
        in_specs=[
            whole(2 * tok, rows),
            pl.BlockSpec((rows, half), lambda i: (0, i)),
            pl.BlockSpec((tok, half), lambda i: (0, i)),
        ],
        out_specs=pl.BlockSpec((tok, half), lambda i: (0, i)),
        out_shape=shape((tok, width)),
        compiler_params=params(1),
    )(cmain, main, total)


def solution(mesh):
    placed = (
        P(AXES, None),
        P(AXES, None),
        P(AXES, None),
        P(),
        P(AXES, None, None),
        P(AXES, None, None),
        P(AXES, None, None),
    )
    return jax.shard_map(on_device, mesh=mesh, in_specs=placed, out_specs=P(AXES, None), check_vma=False)
```

time: 329 us -> 315 us (0.957)
  waiting for transfers between devices: 229 us -> 94.6 us
  blocking collectives: 0 us -> 128 us
  starting transfers between devices: 27.4 us -> 20.5 us
    all_to_all x1 -> x0, waiting for transfers between devices: 130 us -> none  [on_device(): back = exchange(buf)]
    all_to_all x0 -> x1, blocking collectives: none -> 128 us  [on_device(): got = exchange(sent)]
    all_to_all x1 -> x0, starting transfers between devices: 10.2 us -> none  [on_device(): back = exchange(buf)]
    all_to_all x1, waiting for transfers between devices: 98.7 us -> 94.6 us  [on_device(): main = exchange(main.reshape(slots, 8, width)).reshape(rows, width)]
    all_to_all x1, starting transfers between devices: 6.69 us -> 10.3 us  [on_device(): over = exchange(over.reshape(slots, 8, wide)).reshape(rows, wide)]
    pallas_call x3 -> x4, Pallas kernels: 24.2 us -> 24.1 us  [the longest x1 8.75 us: on_device(): pl.pallas_call(combine_main_kernel, name='combine_main', grid=(8,), in_sp...]
  transfers between devices with their start and end apart: 3 -> 2, of which waited for: 2 -> 1; matrix products, arithmetic and copies ran while one was open for 1% -> 1% of each run, Pallas kernels for 10% -> 11%
where the time goes in v2:
time: 315 us; the launch traced here: 314 us
  blocking collectives  128 us (41%)
  waiting for transfers between devices  94.6 us (30%)
  Pallas kernels  66.4 us (21%)
  starting transfers between devices  20.5 us (7%)
  local copies, waits for them, and re-layouts  3.52 us (1%)
    all_to_all x1, blocking collectives, on_device(): got = exchange(sent)  128 us
    all_to_all x1, waiting for transfers between devices, on_device(): main = exchange(main.reshape(slots, 8, width)).reshape(rows, width)  94.6 us
    pallas_call x1, Pallas kernels, on_device(): pl.pallas_call(ffn_main_kernel, name='ffn_main', grid=(8,), in_specs=[pl....  26.8 us
    pallas_call x1, Pallas kernels, on_device(): pl.pallas_call(ffn_over_kernel, name='ffn_over', grid=(8,), in_specs=[pl....  15.5 us
    all_to_all x1, starting transfers between devices, on_device(): over = exchange(over.reshape(slots, 8, wide)).reshape(rows, wide)  10.3 us
    all_to_all x1, starting transfers between devices, on_device(): main = exchange(main.reshape(slots, 8, width)).reshape(rows, width)  10.2 us
    pallas_call x1, Pallas kernels, on_device(): pl.pallas_call(combine_main_kernel, name='combine_main', grid=(8,), in_sp...  8.75 us
    pallas_call x1, Pallas kernels, on_device(): pl.pallas_call(pack_kernel, name='pack', grid=(5,), in_specs=[whole(route...  8.48 us
  transfers between devices with their start and end apart: 2, of which 1 were waited for; matrix products, arithmetic and copies ran while one was open for 1% of the time, Pallas kernels for 11%

profile of v2, /device:TPU:103, one launch (start us, length us, event | category | flops | bytes accessed | tf_op | source)
XLA Modules:
  0.0 313.5 jit_solution(18246266876847820566)
XLA Ops:
  0.0 8.5 %pack.1 = bf16[128,40,1024]{2,1,0:T(8,128)(2,1)} custom-call(s32[8,128]{1,0:T(8,128)} %bitcast.10, s32[1,128]{1,0:T(1,128)} %bitcast.11, bf16[128,4096]{1,0:T(8,128)(2,1)} %tok_ref.1), custom_call_target="tpu_custom_call" | custom-call | tf_op jit(solution)/shard_map/pack/pallas_call | solution.py:240
  8.5 128.4 %all_to_all.15.x_ref = bf16[128,40,1024]{2,1,0:T(8,128)(2,1)} all-to-all(bf16[128,40,1024]{2,1,0:T(8,128)(2,1)} %pack.1), channel_id=1, replica_groups=mesh['node'=16,'local'=8] {'node','local'}, dimensions={0} | all-to-all | bytes 20971520 | tf_op jit(solution)/shard_map/all_to_all | solution.py:254
  136.9 15.5 %ffn_over.1 = bf16[1024,1024]{1,0:T(8,128)(2,1)} custom-call(bf16[128,40,1024]{2,1,0:T(8,128)(2,1)} %all_to_all.15.x_ref, bf16[1,4096,768]{2,1,0:T(8,128)(2,1)} %wg_ref.3, bf16[1,4096,768]{2,1,0:T(8,128)(2,1)} %wu_ref.3, bf16[1,768,4096]{2,1,0:T(8,128)(2,1)} %wd_ref.3), custom_call_target="tpu_custom_call" | custom-call | tf_op jit(solution)/shard_map/ffn_over/pallas_call | solution.py:272
  152.4 10.3 %all-to-all-start.2 = ((bf16[128,8,1024]{2,1,0:T(8,128)(2,1)}), bf16[128,8,1024]{2,1,0:T(8,128)(2,1)S(1)}, u32[]{:S(2)}, u32[]{:S(2)}) async-start(bf16[128,8,1024]{2,1,0:T(8,128)(2,1)} %bitcast.9), calls=%async_computation.2 | async-start | bytes 4194304 | tf_op jit(solution)/shard_map/all_to_all | solution.py:287
  162.8 26.8 %ffn_main.1 = bf16[1024,4096]{1,0:T(8,128)(2,1)} custom-call(bf16[128,40,1024]{2,1,0:T(8,128)(2,1)} %all_to_all.15.x_ref, bf16[1,4096,768]{2,1,0:T(8,128)(2,1)} %wg_ref.3, bf16[1,4096,768]{2,1,0:T(8,128)(2,1)} %wu_ref.3, bf16[1,768,4096]{2,1,0:T(8,128)(2,1)} %wd_ref.3), custom_call_target="tpu_custom_call" | custom-call | tf_op jit(solution)/shard_map/ffn_main/pallas_call | solution.py:288
  189.6 0.0 all-to-all-done.2
  189.6 0.0 copy-start
  189.6 0.0 copy-start.1
  189.6 0.0 copy-start.3
  189.6 0.0 copy-start.2
  189.6 1.3 copy-done
  191.0 10.2 %all-to-all-start.1 = ((bf16[128,8,4096]{2,1,0:T(8,128)(2,1)}), bf16[128,8,4096]{2,1,0:T(8,128)(2,1)}, u32[]{:S(2)}, u32[]{:S(2)}) async-start(bf16[128,8,4096]{2,1,0:T(8,128)(2,1)} %bitcast.7), calls=%async_computation.1 | async-start | bytes 16777216 | tf_op jit(solution)/shard_map/all_to_all | solution.py:298
  201.2 0.0 copy-done.1
  201.2 0.7 copy.8.routes_ref
  201.9 0.0 copy-done.3
  201.9 0.7 copy.10.place_ref
  202.7 0.0 copy-done.2
  202.7 0.7 copy.9.gates_ref
  203.4 2.6 weights.1
  206.0 4.2 %combine_over.1.over_ref = f32[128,4096]{1,0:T(8,128)} custom-call(bf16[256,256]{1,0:T(8,128)(2,1)} %get-tuple-element.8.cover_ref, bf16[1024,1024]{1,0:T(8,128)(2,1)} %bitcast.8), custom_call_target="tpu_custom_call" | custom-call | tf_op jit(solution)/shard_map/combine_over/pallas_call | solution.py:300
  210.2 94.6 %all-to-all-done.1 = bf16[128,8,4096]{2,1,0:T(8,128)(2,1)} async-done(((bf16[128,8,4096]{2,1,0:T(8,128)(2,1)}), bf16[128,8,4096]{2,1,0:T(8,128)(2,1)}, u32[]{:S(2)}, u32[]{:S(2)}) %all-to-all-start.1) | async-done | bytes 8388640 | tf_op jit(solution)/shard_map/all_to_all | solution.py:298
  304.8 8.7 %combine_main.1 = bf16[128,4096]{1,0:T(8,128)(2,1)} custom-call(bf16[256,1024]{1,0:T(8,128)(2,1)} %get-tuple-element.7.cmain_ref, bf16[1024,4096]{1,0:T(8,128)(2,1)} %bitcast.4.main_ref, f32[128,4096]{1,0:T(8,128)} %combine_over.1.over_ref), custom_call_target="tpu_custom_call" | custom-call | tf_op jit(solution)/shard_map/combine_main/pallas_call | solution.py:310
Async XLA Ops:
  152.4 37.2 %all-to-all-start.2 = ((bf16[128,8,1024]{2,1,0:T(8,128)(2,1)}), bf16[128,8,1024]{2,1,0:T(8,128)(2,1)S(1)}, u32[]{:S(2)}, u32[]{:S(2)}) async-start(bf16[128,8,1024]{2,1,0:T(8,128)(2,1)} %bitcast.9), calls=%async_computation.2 | async-start | bytes 4194304 | tf_op jit(solution)/shard_map/all_to_all | solution.py:287
  189.6 1.4 copy-start
  189.6 11.6 %copy-start.1 = (s32[128,8]{0,1:T(8,128)S(1)}, s32[128,8]{0,1:T(8,128)}, u32[]{:S(2)}) copy-start(s32[128,8]{0,1:T(8,128)} %param.8) | copy-start | bytes 12292
  189.6 12.3 %copy-start.3 = (s32[128]{0:T(128)S(1)}, s32[128]{0:T(128)}, u32[]{:S(2)}) copy-start(s32[128]{0:T(128)} %param.10) | copy-start | bytes 1540
  189.6 13.0 %copy-start.2 = (f32[128,8]{0,1:T(8,128)S(1)}, f32[128,8]{0,1:T(8,128)}, u32[]{:S(2)}) copy-start(f32[128,8]{0,1:T(8,128)} %param.9) | copy-start | bytes 12292
  191.0 113.8 %all-to-all-start.1 = ((bf16[128,8,4096]{2,1,0:T(8,128)(2,1)}), bf16[128,8,4096]{2,1,0:T(8,128)(2,1)}, u32[]{:S(2)}, u32[]{:S(2)}) async-start(bf16[128,8,4096]{2,1,0:T(8,128)(2,1)} %bitcast.7), calls=%async_computation.1 | async-start | bytes 16777216 | tf_op jit(solution)/shard_map/all_to_all | solution.py:298

commit v3 on v2

v3 whole, which is shorter than its diff:
```python
import functools

import jax
import jax.numpy as jnp
from jax import lax
from jax.experimental import pallas as pl
from jax.experimental.pallas import tpu as pltpu
from jax.sharding import PartitionSpec as P

AXES = ("node", "local")
F32 = jnp.float32
BF16 = jnp.bfloat16


def iota(shape, dim):
    return lax.broadcasted_iota(jnp.int32, shape, dim)


def dot(a, b):
    return jnp.dot(a, b, preferred_element_type=F32)


def rank_by_slot(routes_t, place_row):
    top, tok = routes_t.shape
    slots = place_row.shape[1]
    rows = iota((slots, tok), 0)
    chosen = jnp.zeros((slots, tok), F32)
    for k in range(top):
        chosen = chosen + (routes_t[k : k + 1, :] == rows).astype(F32)
    perm = (place_row == iota((slots, slots), 0)).astype(F32).astype(BF16)
    at_slot = dot(perm, chosen.astype(BF16))
    before = (iota((tok, tok), 0) < iota((tok, tok), 1)).astype(F32).astype(BF16)
    rank = dot(at_slot.astype(BF16), before)
    return jnp.where(at_slot > 0.5, rank, -1.0)


GROUP = 32


def regroup(back):
    size = GROUP * 8
    grouped, plain = iota((size, size), 1 if back else 0), iota((size, size), 0 if back else 1)
    return (plain == grouped % GROUP * 8 + grouped // GROUP).astype(F32).astype(BF16)


def pack_kernel(routes_ref, place_ref, tok_ref, out_ref, buf_ref, part_ref, sems):
    tok, width = tok_ref.shape
    slots = place_ref.shape[1]
    groups = slots // GROUP
    wide = width // 4
    pair = GROUP * 2
    key = rank_by_slot(routes_ref[...], place_ref[...])
    hit = key[:, None, :] == iota((slots, 8, tok), 1).astype(F32)
    sel = hit.astype(F32).reshape(slots * 8, tok).astype(BF16)
    copies = []

    def send(q, lo, hi, value):
        buf_ref[lo:hi, q * 8 : (q + 1) * 8, :] = value.reshape(hi - lo, 8, wide).astype(BF16)
        here = (slice(lo, hi), slice(q * 8, (q + 1) * 8))
        copy = pltpu.make_async_copy(buf_ref.at[here], out_ref.at[here], sems.at[len(copies)])
        copy.start()
        copies.append(copy)

    half = slots // 2
    for q in range(4):
        for lo in (0, half):
            rows = sel[lo * 8 : (lo + half) * 8]
            send(q, lo, lo + half, dot(rows, tok_ref[:, q * wide : (q + 1) * wide]))
    sel = jnp.concatenate(
        [
            (key[g * GROUP : (g + 1) * GROUP, :] == 8.0 + r).astype(F32)
            for g in range(groups)
            for r in range(2)
        ],
        axis=0,
    ).astype(BF16)
    for q in range(4):
        out = dot(sel, tok_ref[:, q * wide : (q + 1) * wide]).astype(BF16)
        for g in range(groups):
            part_ref[g, q * pair : (q + 1) * pair, :] = out[g * pair : (g + 1) * pair]
    order = regroup(True)
    for g in range(groups):
        send(4, g * GROUP, (g + 1) * GROUP, dot(order, part_ref[g]))
    for copy in copies:
        copy.wait()


def silu_mul(gate, up):
    return (gate / (1.0 + jnp.exp(-gate)) * up).astype(BF16)


class Queue:
    def __init__(self, copies, depth):
        self.copies, self.depth, self.done = copies, depth, 0
        for copy in copies[:depth]:
            copy.start()

    def next(self):
        self.copies[self.done].wait()
        self.done += 1
        if self.done + self.depth <= len(self.copies):
            self.copies[self.done + self.depth - 1].start()


def ffn_main_kernel(
    got_ref,
    wg_hbm,
    wu_hbm,
    wd_hbm,
    out_ref,
    x_ref,
    wg_ref,
    wu_ref,
    wd_ref,
    gate_ref,
    up_ref,
    hid_ref,
    back_ref,
    in_sems,
    out_sems,
):
    rows, width = back_ref.shape
    wide = width // 4
    block = 512
    blocks = [slice(m, m + block) for m in range(0, rows, block)]
    quarters = [slice(q * wide, (q + 1) * wide) for q in range(4)]
    sem = iter(range(16))
    copies = []
    for q, p in enumerate(quarters):
        copies.append(pltpu.make_async_copy(got_ref.at[:, 8 * q : 8 * q + 8, :], x_ref.at[q], in_sems.at[next(sem)]))
        copies.append(pltpu.make_async_copy(wg_hbm.at[0, p, :], wg_ref.at[p, :], in_sems.at[next(sem)]))
        copies.append(pltpu.make_async_copy(wu_hbm.at[0, p, :], wu_ref.at[p, :], in_sems.at[next(sem)]))
    for p in quarters:
        copies.append(pltpu.make_async_copy(wd_hbm.at[0, :, p], wd_ref.at[:, p], in_sems.at[next(sem)]))
    queue = Queue(copies, 5)
    for q, p in enumerate(quarters):
        for _ in range(3):
            queue.next()
        for m in blocks:
            x = x_ref[q, m.start // 8 : m.stop // 8].reshape(block, wide)
            gate = dot(x, wg_ref[p, :])
            up = dot(x, wu_ref[p, :])
            if q:
                gate = gate + gate_ref[m, :]
                up = up + up_ref[m, :]
            if q < 3:
                gate_ref[m, :] = gate
                up_ref[m, :] = up
            else:
                hid_ref[m, :] = silu_mul(gate, up)
    give = []
    for p in quarters:
        queue.next()
        for m in blocks:
            back_ref[m, p] = dot(hid_ref[m, :], wd_ref[:, p]).astype(BF16)
            copy = pltpu.make_async_copy(back_ref.at[m, p], out_ref.at[m, p], out_sems.at[len(give)])
            copy.start()
            give.append(copy)
    for copy in give:
        copy.wait()


def ffn_over_kernel(
    got_ref, wg_hbm, wu_hbm, wd_hbm, out_ref, x_ref, wg_ref, wu_ref, wd_ref, part_ref, back_ref, in_sems, w_sems, out_sems
):
    groups = part_ref.shape[0]
    wide = x_ref.shape[2]
    size = GROUP * 8
    pair = GROUP * 2
    quarters = [slice(q * wide, (q + 1) * wide) for q in range(4)]
    slots = [slice(g * GROUP, (g + 1) * GROUP) for g in range(groups)]
    lines = [slice(g * size, (g + 1) * size) for g in range(groups)]
    take = [pltpu.make_async_copy(got_ref.at[s, 32:40, :], x_ref.at[s], in_sems.at[g]) for g, s in enumerate(slots)]
    give = [pltpu.make_async_copy(back_ref.at[r, :], out_ref.at[r, :], out_sems.at[g]) for g, r in enumerate(lines)]
    gates = [pltpu.make_async_copy(wg_hbm.at[0, p, :], wg_ref.at[p, :], w_sems.at[q]) for q, p in enumerate(quarters)]
    ups = [pltpu.make_async_copy(wu_hbm.at[0, p, :], wu_ref.at[p, :], w_sems.at[4 + q]) for q, p in enumerate(quarters)]
    downs = [pltpu.make_async_copy(wd_hbm.at[0, :, p], wd_ref.at[:, p], w_sems.at[8 + q]) for q, p in enumerate(quarters)]
    queue = Queue(take + [c for pair_of in zip(gates, ups) for c in pair_of] + downs, 5)
    order = regroup(False)
    for g in range(groups):
        queue.next()
        part_ref[g] = dot(order, x_ref[slots[g]].reshape(size, wide)).astype(BF16)
    gate = up = None
    for q, p in enumerate(quarters):
        x = jnp.concatenate([part_ref[g, q * pair : (q + 1) * pair, :] for g in range(groups)], axis=0)
        queue.next()
        one = dot(x, wg_ref[p, :])
        queue.next()
        two = dot(x, wu_ref[p, :])
        gate, up = (one, two) if q == 0 else (gate + one, up + two)
    hidden = silu_mul(gate, up)
    for q, p in enumerate(quarters):
        queue.next()
        out = dot(hidden, wd_ref[:, p]).astype(BF16)
        for g in range(groups):
            part_ref[g, q * pair : (q + 1) * pair, :] = out[g * pair : (g + 1) * pair]
    order = regroup(True)
    for g in range(groups):
        back_ref[lines[g], :] = dot(order, part_ref[g]).astype(BF16)
        give[g].start()
    for copy in give:
        copy.wait()


def weights_kernel(routes_ref, gates_ref, place_ref, cmain_ref, cover_ref):
    tok, top = routes_ref.shape
    slots = place_ref.shape[0]
    lanes = iota((tok, slots), 1)
    chosen = jnp.zeros((tok, slots), F32)
    weight = jnp.zeros((tok, slots), F32)
    for k in range(top):
        hit = (routes_ref[:, k : k + 1] == lanes).astype(F32)
        chosen = chosen + hit
        weight = weight + hit * gates_ref[:, k : k + 1]
    perm = (place_ref[...] == iota((slots, slots), 1)).astype(F32).astype(BF16)
    high = weight.astype(BF16)
    low = (weight - high.astype(F32)).astype(BF16)
    at_slot = dot(chosen.astype(BF16), perm)
    before = (iota((tok, tok), 1) < iota((tok, tok), 0)).astype(F32).astype(BF16)
    rank = dot(before, at_slot.astype(BF16))
    key = jnp.where(at_slot > 0.5, rank, -1.0).astype(BF16)
    high = dot(high, perm).astype(BF16)
    low = dot(low, perm).astype(BF16)

    def place(out_ref, slot_of, rank_of):
        width = out_ref.shape[1]
        lane = iota((slots, width), 1)
        spread = (slot_of(lane) == iota((slots, width), 0)).astype(F32).astype(BF16)
        hit = dot(key, spread) == rank_of(iota((tok, width), 1)).astype(F32)
        out_ref[:tok, :] = jnp.where(hit, dot(high, spread), 0.0).astype(BF16)
        out_ref[tok:, :] = jnp.where(hit, dot(low, spread), 0.0).astype(BF16)

    place(cmain_ref, lambda i: i // 8, lambda i: i % 8)
    place(cover_ref, lambda i: i // (2 * GROUP) * GROUP + i % GROUP, lambda i: 8 + i // GROUP % 2)


def combine_over_kernel(cover_ref, over_ref, out_ref):
    tok = out_ref.shape[0]
    wide = over_ref.shape[1]
    size = GROUP * 8
    pair = GROUP * 2
    order = regroup(False)
    parts = [
        dot(order, over_ref[i : i + size, :]).astype(BF16) for i in range(0, over_ref.shape[0], size)
    ]
    for q in range(4):
        over = jnp.concatenate([part[q * pair : (q + 1) * pair] for part in parts], axis=0)
        total = dot(cover_ref[...], over)
        out_ref[:, q * wide : (q + 1) * wide] = total[:tok] + total[tok:]


COLUMNS = (1024, 1024, 1024, 512, 512)


def combine_main_kernel(
    cmain_hbm, over_hbm, main_ref, out_ref, cmain_ref, over_ref, x_ref, y_ref, in_sems, over_sems, out_sems, cmain_sem
):
    tok = y_ref.shape[0]
    starts = [sum(COLUMNS[:i]) for i in range(len(COLUMNS))]
    parts = [slice(a, a + n) for a, n in zip(starts, COLUMNS)]
    coefs = pltpu.make_async_copy(cmain_hbm, cmain_ref, cmain_sem)
    take = [pltpu.make_async_copy(main_ref.at[:, p], x_ref.at[:, p], in_sems.at[i]) for i, p in enumerate(parts)]
    more = [pltpu.make_async_copy(over_hbm.at[:, p], over_ref.at[:, p], over_sems.at[i]) for i, p in enumerate(parts)]
    give = [pltpu.make_async_copy(y_ref.at[:, p], out_ref.at[:, p], out_sems.at[i]) for i, p in enumerate(parts)]
    queue = Queue([coefs] + [c for pair_of in zip(take, more) for c in pair_of], 5)
    queue.next()
    for i, p in enumerate(parts):
        queue.next()
        total = dot(cmain_ref[...], x_ref[:, p])
        queue.next()
        y_ref[:, p] = (total[:tok] + total[tok:] + over_ref[:, p]).astype(BF16)
        give[i].start()
    for copy in give:
        copy.wait()


def params(grid_dims, mib=60):
    return pltpu.CompilerParams(dimension_semantics=("arbitrary",) * grid_dims if grid_dims else None, vmem_limit_bytes=mib << 20)


def shape(dims, kind=BF16):
    return jax.ShapeDtypeStruct(dims, kind)


def on_device(tokens, routes, gates, placement, w_gate, w_up, w_down):
    tok, width = tokens.shape
    slots = placement.shape[0]
    hid = w_gate.shape[2]
    rows = slots * 8
    wide = width // 4
    exchange = functools.partial(lax.all_to_all, axis_name=AXES, split_axis=0, concat_axis=0, tiled=True)
    whole = lambda *dims: pl.BlockSpec(dims, lambda *_: (0,) * len(dims))

    hbm = pl.BlockSpec(memory_space=pl.ANY)
    sent = pl.pallas_call(
        pack_kernel,
        name="pack",
        grid=(1,),
        in_specs=[whole(routes.shape[1], tok), whole(1, slots), whole(tok, width)],
        out_specs=hbm,
        out_shape=shape((slots, 40, wide)),
        scratch_shapes=[
            pltpu.VMEM((slots, 40, wide), BF16),
            pltpu.VMEM((slots // GROUP, 8 * GROUP, wide), BF16),
            pltpu.SemaphoreType.DMA((8 + slots // GROUP,)),
        ],
        compiler_params=params(0),
    )(routes.T, placement.reshape(1, slots), tokens)
    got = exchange(sent)
    cmain, cover = pl.pallas_call(
        weights_kernel,
        name="weights",
        grid=(1,),
        in_specs=[whole(tok, routes.shape[1]), whole(tok, routes.shape[1]), whole(slots, 1)],
        out_specs=[whole(2 * tok, rows), whole(2 * tok, 2 * slots)],
        out_shape=[shape((2 * tok, rows)), shape((2 * tok, 2 * slots))],
        compiler_params=params(1),
    )(routes, gates, placement.reshape(slots, 1))

    over = pl.pallas_call(
        ffn_over_kernel,
        name="ffn_over",
        in_specs=[hbm] * 4,
        out_specs=hbm,
        out_shape=shape((rows, wide)),
        scratch_shapes=[
            pltpu.VMEM((slots, 8, wide), BF16),
            pltpu.VMEM((width, hid), BF16),
            pltpu.VMEM((width, hid), BF16),
            pltpu.VMEM((hid, width), BF16),
            pltpu.VMEM((slots // GROUP, 8 * GROUP, wide), BF16),
            pltpu.VMEM((rows, wide), BF16),
            pltpu.SemaphoreType.DMA((slots // GROUP,)),
            pltpu.SemaphoreType.DMA((12,)),
            pltpu.SemaphoreType.DMA((slots // GROUP,)),
        ],
        compiler_params=params(0),
    )(got, w_gate, w_up, w_down)
    over = exchange(over.reshape(slots, 8, wide)).reshape(rows, wide)
    main = pl.pallas_call(
        ffn_main_kernel,
        name="ffn_main",
        in_specs=[hbm] * 4,
        out_specs=hbm,
        out_shape=shape((rows, width)),
        scratch_shapes=[
            pltpu.VMEM((4, slots, 8, wide), BF16),
            pltpu.VMEM((width, hid), BF16),
            pltpu.VMEM((width, hid), BF16),
            pltpu.VMEM((hid, width), BF16),
            pltpu.VMEM((rows, hid), F32),
            pltpu.VMEM((rows, hid), F32),
            pltpu.VMEM((rows, hid), BF16),
            pltpu.VMEM((rows, width), BF16),
            pltpu.SemaphoreType.DMA((16,)),
            pltpu.SemaphoreType.DMA((4 * rows // 512,)),
        ],
        compiler_params=params(0),
    )(got, w_gate, w_up, w_down)
    main = exchange(main.reshape(slots, 8, width)).reshape(rows, width)

    total = pl.pallas_call(
        combine_over_kernel,
        name="combine_over",
        grid=(1,),
        in_specs=[whole(2 * tok, 2 * slots), whole(rows, wide)],
        out_specs=whole(tok, width),
        out_shape=shape((tok, width), F32),
        compiler_params=params(1),
    )(cover, over)
    return pl.pallas_call(
        combine_main_kernel,
        name="combine_main",
        in_specs=[hbm] * 3,
        out_specs=hbm,
        out_shape=shape((tok, width)),
        scratch_shapes=[
            pltpu.VMEM((2 * tok, rows), BF16),
            pltpu.VMEM((tok, width), F32),
            pltpu.VMEM((rows, width), BF16),
            pltpu.VMEM((tok, width), BF16),
            pltpu.SemaphoreType.DMA((len(COLUMNS),)),
            pltpu.SemaphoreType.DMA((len(COLUMNS),)),
            pltpu.SemaphoreType.DMA((len(COLUMNS),)),
            pltpu.SemaphoreType.DMA,
        ],
        compiler_params=params(0),
    )(cmain, total, main)


def solution(mesh):
    placed = (
        P(AXES, None),
        P(AXES, None),
        P(AXES, None),
        P(),
        P(AXES, None, None),
        P(AXES, None, None),
        P(AXES, None, None),
    )
    return jax.shard_map(on_device, mesh=mesh, in_specs=placed, out_specs=P(AXES, None), check_vma=False)
```

time: 315 us -> 306 us (0.971)
  Pallas kernels: 66.4 us -> 55.7 us
    pallas_call x4, Pallas kernels: 59.6 us -> 48.8 us  [the longest x1 24.9 us: on_device(): pl.pallas_call(ffn_main_kernel, name='ffn_main', in_specs=[hbm] * 4, out_...]
  transfers between devices with their start and end apart: 2 -> 2, of which waited for: 1 -> 2; matrix products, arithmetic and copies ran while one was open for 1% -> 1% of each run, Pallas kernels for 11% -> 10%
where the time goes in v3:
time: 306 us; the launch traced here: 305 us
  blocking collectives  128 us (42%)
  waiting for transfers between devices  96.4 us (32%)
  Pallas kernels  55.7 us (18%)
  starting transfers between devices  21.1 us (7%)
  local copies, waits for them, and re-layouts  3.55 us (1%)
    all_to_all x1, blocking collectives, on_device(): got = exchange(sent)  128 us
    all_to_all x1, waiting for transfers between devices, on_device(): main = exchange(main.reshape(slots, 8, width)).reshape(rows, width)  95.7 us
    pallas_call x1, Pallas kernels, on_device(): pl.pallas_call(ffn_main_kernel, name='ffn_main', in_specs=[hbm] * 4, out_...  24.9 us
    pallas_call x1, Pallas kernels, on_device(): pl.pallas_call(ffn_over_kernel, name='ffn_over', in_specs=[hbm] * 4, out_...  11.6 us
    all_to_all x1, starting transfers between devices, on_device(): main = exchange(main.reshape(slots, 8, width)).reshape(rows, width)  10.6 us
    all_to_all x1, starting transfers between devices, on_device(): over = exchange(over.reshape(slots, 8, wide)).reshape(rows, wide)  10.5 us
    pallas_call x1, Pallas kernels, on_device(): pl.pallas_call(combine_main_kernel, name='combine_main', in_specs=[hbm] *...  6.15 us
    pallas_call x1, Pallas kernels, on_device(): pl.pallas_call(pack_kernel, name='pack', grid=(1,), in_specs=[whole(route...  6.14 us
  transfers between devices with their start and end apart: 2, of which 2 were waited for; matrix products, arithmetic and copies ran while one was open for 1% of the time, Pallas kernels for 10%

profile of v3, /device:TPU:103, one launch (start us, length us, event | category | flops | bytes accessed | tf_op | source)
XLA Modules:
  0.0 305.4 jit_solution(9773726514889817472)
XLA Ops:
  0.0 6.1 %pack.1 = bf16[128,40,1024]{2,1,0:T(8,128)(2,1)} custom-call(s32[8,128]{1,0:T(8,128)} %bitcast.10, s32[1,128]{1,0:T(1,128)} %bitcast.11, bf16[128,4096]{1,0:T(8,128)(2,1)} %tok_ref.1), custom_call_target="tpu_custom_call" | custom-call | tf_op jit(solution)/shard_map/pack/pallas_call | solution.py:295
  6.2 128.4 %all_to_all.15.got_ref = bf16[128,40,1024]{2,1,0:T(8,128)(2,1)} all-to-all(bf16[128,40,1024]{2,1,0:T(8,128)(2,1)} %pack.1), channel_id=1, replica_groups=mesh['node'=16,'local'=8] {'node','local'}, dimensions={0} | all-to-all | bytes 20971520 | tf_op jit(solution)/shard_map/all_to_all | solution.py:309
  134.6 11.6 %ffn_over.1 = bf16[1024,1024]{1,0:T(8,128)(2,1)} custom-call(bf16[128,40,1024]{2,1,0:T(8,128)(2,1)} %all_to_all.15.got_ref, bf16[1,4096,768]{2,1,0:T(8,128)(2,1)} %wg_hbm.3, bf16[1,4096,768]{2,1,0:T(8,128)(2,1)} %wu_hbm.3, bf16[1,768,4096]{2,1,0:T(8,128)(2,1)} %wd_hbm.3), custom_call_target="tpu_custom_call" | custom-call | tf_op jit(solution)/shard_map/ffn_over/pallas_call | solution.py:320
  146.2 10.5 %all-to-all-start.1 = ((bf16[128,8,1024]{2,1,0:T(8,128)(2,1)}), bf16[128,8,1024]{2,1,0:T(8,128)(2,1)S(1)}, u32[]{:S(2)}, u32[]{:S(2)}) async-start(bf16[128,8,1024]{2,1,0:T(8,128)(2,1)} %bitcast.9), calls=%async_computation.1 | async-start | bytes 4194304 | tf_op jit(solution)/shard_map/all_to_all | solution.py:339
  156.7 24.9 %ffn_main.1 = bf16[1024,4096]{1,0:T(8,128)(2,1)} custom-call(bf16[128,40,1024]{2,1,0:T(8,128)(2,1)} %all_to_all.15.got_ref, bf16[1,4096,768]{2,1,0:T(8,128)(2,1)} %wg_hbm.3, bf16[1,4096,768]{2,1,0:T(8,128)(2,1)} %wu_hbm.3, bf16[1,768,4096]{2,1,0:T(8,128)(2,1)} %wd_hbm.3), custom_call_target="tpu_custom_call" | custom-call | tf_op jit(solution)/shard_map/ffn_main/pallas_call | solution.py:340
  181.7 0.7 all-to-all-done.1
  182.3 0.0 copy-start
  182.3 0.0 copy-start.1
  182.3 0.0 copy-start.3
  182.4 0.0 copy-start.2
  182.4 1.4 copy-done
  183.7 10.6 %all-to-all-start.2 = ((bf16[128,8,4096]{2,1,0:T(8,128)(2,1)}), bf16[128,8,4096]{2,1,0:T(8,128)(2,1)}, u32[]{:S(2)}, u32[]{:S(2)}) async-start(bf16[128,8,4096]{2,1,0:T(8,128)(2,1)} %bitcast.7), calls=%async_computation.2 | async-start | bytes 16777216 | tf_op jit(solution)/shard_map/all_to_all | solution.py:360
  194.4 0.0 copy-done.1
  194.4 0.7 copy.8.routes_ref
  195.1 0.0 copy-done.3
  195.1 0.7 copy.10.place_ref
  195.8 0.0 copy-done.2
  195.8 0.7 copy.9.gates_ref
  196.5 2.6 weights.1
  199.2 4.2 %combine_over.1.over_hbm = f32[128,4096]{1,0:T(8,128)} custom-call(bf16[256,256]{1,0:T(8,128)(2,1)} %get-tuple-element.8.cover_ref, bf16[1024,1024]{1,0:T(8,128)(2,1)} %bitcast.8), custom_call_target="tpu_custom_call" | custom-call | tf_op jit(solution)/shard_map/combine_over/pallas_call | solution.py:362
  203.4 95.7 %all-to-all-done.2 = bf16[128,8,4096]{2,1,0:T(8,128)(2,1)} async-done(((bf16[128,8,4096]{2,1,0:T(8,128)(2,1)}), bf16[128,8,4096]{2,1,0:T(8,128)(2,1)}, u32[]{:S(2)}, u32[]{:S(2)}) %all-to-all-start.2) | async-done | bytes 8388640 | tf_op jit(solution)/shard_map/all_to_all | solution.py:360
  299.1 6.1 %combine_main.1 = bf16[128,4096]{1,0:T(8,128)(2,1)} custom-call(bf16[256,1024]{1,0:T(8,128)(2,1)} %get-tuple-element.7.cmain_hbm, f32[128,4096]{1,0:T(8,128)} %combine_over.1.over_hbm, bf16[1024,4096]{1,0:T(8,128)(2,1)} %bitcast.6.main_ref), custom_call_target="tpu_custom_call" | custom-call | tf_op jit(solution)/shard_map/combine_main/pallas_call | solution.py:371
Async XLA Ops:
  146.2 36.1 %all-to-all-start.1 = ((bf16[128,8,1024]{2,1,0:T(8,128)(2,1)}), bf16[128,8,1024]{2,1,0:T(8,128)(2,1)S(1)}, u32[]{:S(2)}, u32[]{:S(2)}) async-start(bf16[128,8,1024]{2,1,0:T(8,128)(2,1)} %bitcast.9), calls=%async_computation.1 | async-start | bytes 4194304 | tf_op jit(solution)/shard_map/all_to_all | solution.py:339
  182.3 1.4 copy-start
  182.3 12.0 %copy-start.1 = (s32[128,8]{0,1:T(8,128)S(1)}, s32[128,8]{0,1:T(8,128)}, u32[]{:S(2)}) copy-start(s32[128,8]{0,1:T(8,128)} %param.8) | copy-start | bytes 12292
  182.3 12.7 %copy-start.3 = (s32[128]{0:T(128)S(1)}, s32[128]{0:T(128)}, u32[]{:S(2)}) copy-start(s32[128]{0:T(128)} %param.10) | copy-start | bytes 1540
  182.4 13.5 %copy-start.2 = (f32[128,8]{0,1:T(8,128)S(1)}, f32[128,8]{0,1:T(8,128)}, u32[]{:S(2)}) copy-start(f32[128,8]{0,1:T(8,128)} %param.9) | copy-start | bytes 12292
  183.7 115.4 %all-to-all-start.2 = ((bf16[128,8,4096]{2,1,0:T(8,128)(2,1)}), bf16[128,8,4096]{2,1,0:T(8,128)(2,1)}, u32[]{:S(2)}, u32[]{:S(2)}) async-start(bf16[128,8,4096]{2,1,0:T(8,128)(2,1)} %bitcast.7), calls=%async_computation.2 | async-start | bytes 16777216 | tf_op jit(solution)/shard_map/all_to_all | solution.py:360

commit v4 on v3

--- a/solution.py
+++ b/solution.py
@@ -43,7 +43,7 @@
     return (plain == grouped % GROUP * 8 + grouped // GROUP).astype(F32).astype(BF16)
 
 
-def pack_kernel(routes_ref, place_ref, tok_ref, out_ref, buf_ref, part_ref, sems):
+def pack_kernel(routes_ref, place_ref, tok_ref, out_ref, part_ref):
     tok, width = tok_ref.shape
     slots = place_ref.shape[1]
     groups = slots // GROUP
@@ -52,14 +52,9 @@
     key = rank_by_slot(routes_ref[...], place_ref[...])
     hit = key[:, None, :] == iota((slots, 8, tok), 1).astype(F32)
     sel = hit.astype(F32).reshape(slots * 8, tok).astype(BF16)
-    copies = []
 
     def send(q, lo, hi, value):
-        buf_ref[lo:hi, q * 8 : (q + 1) * 8, :] = value.reshape(hi - lo, 8, wide).astype(BF16)
-        here = (slice(lo, hi), slice(q * 8, (q + 1) * 8))
-        copy = pltpu.make_async_copy(buf_ref.at[here], out_ref.at[here], sems.at[len(copies)])
-        copy.start()
-        copies.append(copy)
+        out_ref[lo:hi, q * 8 : (q + 1) * 8, :] = value.reshape(hi - lo, 8, wide).astype(BF16)
 
     half = slots // 2
     for q in range(4):
@@ -81,8 +76,6 @@
     order = regroup(True)
     for g in range(groups):
         send(4, g * GROUP, (g + 1) * GROUP, dot(order, part_ref[g]))
-    for copy in copies:
-        copy.wait()
 
 
 def silu_mul(gate, up):
@@ -161,7 +154,7 @@
 
 
 def ffn_over_kernel(
-    got_ref, wg_hbm, wu_hbm, wd_hbm, out_ref, x_ref, wg_ref, wu_ref, wd_ref, part_ref, back_ref, in_sems, w_sems, out_sems
+    got_ref, wg_ref, wu_ref, wd_hbm, out_ref, x_ref, wd_ref, part_ref, back_ref, in_sems, out_sems
 ):
     groups = part_ref.shape[0]
     wide = x_ref.shape[2]
@@ -172,10 +165,10 @@
     lines = [slice(g * size, (g + 1) * size) for g in range(groups)]
     take = [pltpu.make_async_copy(got_ref.at[s, 32:40, :], x_ref.at[s], in_sems.at[g]) for g, s in enumerate(slots)]
     give = [pltpu.make_async_copy(back_ref.at[r, :], out_ref.at[r, :], out_sems.at[g]) for g, r in enumerate(lines)]
-    gates = [pltpu.make_async_copy(wg_hbm.at[0, p, :], wg_ref.at[p, :], w_sems.at[q]) for q, p in enumerate(quarters)]
-    ups = [pltpu.make_async_copy(wu_hbm.at[0, p, :], wu_ref.at[p, :], w_sems.at[4 + q]) for q, p in enumerate(quarters)]
-    downs = [pltpu.make_async_copy(wd_hbm.at[0, :, p], wd_ref.at[:, p], w_sems.at[8 + q]) for q, p in enumerate(quarters)]
-    queue = Queue(take + [c for pair_of in zip(gates, ups) for c in pair_of] + downs, 5)
+    downs = [
+        pltpu.make_async_copy(wd_hbm.at[0, :, p], wd_ref.at[:, p], in_sems.at[groups + q]) for q, p in enumerate(quarters)
+    ]
+    queue = Queue(take + downs, 5)
     order = regroup(False)
     for g in range(groups):
         queue.next()
@@ -183,10 +176,8 @@
     gate = up = None
     for q, p in enumerate(quarters):
         x = jnp.concatenate([part_ref[g, q * pair : (q + 1) * pair, :] for g in range(groups)], axis=0)
-        queue.next()
-        one = dot(x, wg_ref[p, :])
-        queue.next()
-        two = dot(x, wu_ref[p, :])
+        one = dot(x, wg_ref[0, p, :])
+        two = dot(x, wu_ref[0, p, :])
         gate, up = (one, two) if q == 0 else (gate + one, up + two)
     hidden = silu_mul(gate, up)
     for q, p in enumerate(quarters):
@@ -292,19 +283,15 @@
     whole = lambda *dims: pl.BlockSpec(dims, lambda *_: (0,) * len(dims))
 
     hbm = pl.BlockSpec(memory_space=pl.ANY)
+    vmem = pl.BlockSpec(memory_space=pltpu.VMEM)
     sent = pl.pallas_call(
         pack_kernel,
         name="pack",
-        grid=(1,),
-        in_specs=[whole(routes.shape[1], tok), whole(1, slots), whole(tok, width)],
-        out_specs=hbm,
-        out_shape=shape((slots, 40, wide)),
-        scratch_shapes=[
-            pltpu.VMEM((slots, 40, wide), BF16),
-            pltpu.VMEM((slots // GROUP, 8 * GROUP, wide), BF16),
-            pltpu.SemaphoreType.DMA((8 + slots // GROUP,)),
-        ],
-        compiler_params=params(0),
+        in_specs=[vmem, vmem, vmem],
+        out_specs=vmem,
+        out_shape=pltpu.VMEM((slots, 40, wide), BF16),
+        scratch_shapes=[pltpu.VMEM((slots // GROUP, 8 * GROUP, wide), BF16)],
+        compiler_params=params(0, 48),
     )(routes.T, placement.reshape(1, slots), tokens)
     got = exchange(sent)
     cmain, cover = pl.pallas_call(
@@ -320,21 +307,18 @@
     over = pl.pallas_call(
         ffn_over_kernel,
         name="ffn_over",
-        in_specs=[hbm] * 4,
+        in_specs=[hbm, vmem, vmem, hbm],
         out_specs=hbm,
         out_shape=shape((rows, wide)),
         scratch_shapes=[
             pltpu.VMEM((slots, 8, wide), BF16),
-            pltpu.VMEM((width, hid), BF16),
-            pltpu.VMEM((width, hid), BF16),
             pltpu.VMEM((hid, width), BF16),
             pltpu.VMEM((slots // GROUP, 8 * GROUP, wide), BF16),
             pltpu.VMEM((rows, wide), BF16),
-            pltpu.SemaphoreType.DMA((slots // GROUP,)),
-            pltpu.SemaphoreType.DMA((12,)),
+            pltpu.SemaphoreType.DMA((slots // GROUP + 4,)),
             pltpu.SemaphoreType.DMA((slots // GROUP,)),
         ],
-        compiler_params=params(0),
+        compiler_params=params(0, 36),
     )(got, w_gate, w_up, w_down)
     over = exchange(over.reshape(slots, 8, wide)).reshape(rows, wide)
     main = pl.pallas_call(

time: 306 us -> 302 us (0.987)
  Pallas kernels: 55.7 us -> 52.3 us
    pallas_call x2, Pallas kernels: 17.7 us -> 14.3 us  [the longest x1 9.37 us: on_device(): pl.pallas_call(ffn_over_kernel, name='ffn_over', in_specs=[hbm, vmem, vme...]
  transfers between devices with their start and end apart: 2 -> 2, of which waited for: 2 -> 2; matrix products, arithmetic and copies ran while one was open for 1% -> 1% of each run, Pallas kernels for 10% -> 11%
where the time goes in v4:
time: 302 us
  blocking collectives  128 us (42%)
  waiting for transfers between devices  96.3 us (32%)
  Pallas kernels  52.3 us (17%)
  starting transfers between devices  21.2 us (7%)
  local copies, waits for them, and re-layouts  3.57 us (1%)
    all_to_all x1, blocking collectives, on_device(): got = exchange(sent)  128 us
    all_to_all x1, waiting for transfers between devices, on_device(): main = exchange(main.reshape(slots, 8, width)).reshape(rows, width)  95.7 us
    pallas_call x1, Pallas kernels, on_device(): pl.pallas_call(ffn_main_kernel, name='ffn_main', in_specs=[hbm] * 4, out_...  25 us
    all_to_all x1, starting transfers between devices, on_device(): main = exchange(main.reshape(slots, 8, width)).reshape(rows, width)  10.6 us
    all_to_all x1, starting transfers between devices, on_device(): over = exchange(over.reshape(slots, 8, wide)).reshape(rows, wide)  10.5 us
    pallas_call x1, Pallas kernels, on_device(): pl.pallas_call(ffn_over_kernel, name='ffn_over', in_specs=[hbm, vmem, vme...  9.37 us
    pallas_call x1, Pallas kernels, on_device(): pl.pallas_call(combine_main_kernel, name='combine_main', in_specs=[hbm] *...  6.09 us
  transfers between devices with their start and end apart: 2, of which 2 were waited for; matrix products, arithmetic and copies ran while one was open for 1% of the time, Pallas kernels for 11%

profile of v4, /device:TPU:103, one launch (start us, length us, event | category | flops | bytes accessed | tf_op | source)
XLA Modules:
  0.0 301.8 jit_solution(570999676490049324)
XLA Ops:
  0.0 5.0 %pack.1 = bf16[128,40,1024]{2,1,0:T(8,128)(2,1)S(1)} custom-call(s32[8,128]{1,0:T(8,128)} %bitcast.9, s32[1,128]{1,0:T(1,128)} %bitcast.10, bf16[128,4096]{1,0:T(8,128)(2,1)} %tok_ref.1), custom_call_target="tpu_custom_call" | custom-call | tf_op jit(solution)/shard_map/pack/pallas_call | solution.py:287
  5.0 0.0 copy-start
  5.0 0.0 copy-start.1
  5.0 128.2 %all_to_all.15.got_ref = bf16[128,40,1024]{2,1,0:T(8,128)(2,1)} all-to-all(bf16[128,40,1024]{2,1,0:T(8,128)(2,1)S(1)} %pack.1), channel_id=1, replica_groups=mesh['node'=16,'local'=8] {'node','local'}, dimensions={0} | all-to-all | bytes 20971520 | tf_op jit(solution)/shard_map/all_to_all | solution.py:296
  133.2 0.0 copy-done
  133.2 0.0 copy-done.1
  133.2 9.4 %ffn_over.1 = bf16[1024,1024]{1,0:T(8,128)(2,1)} custom-call(bf16[128,40,1024]{2,1,0:T(8,128)(2,1)} %all_to_all.15.got_ref, bf16[1,4096,768]{2,1,0:T(8,128)(2,1)S(1)} %copy-done, bf16[1,4096,768]{2,1,0:T(8,128)(2,1)S(1)} %copy-done.1, bf16[1,768,4096]{2,1,0:T(8,128)(2,1)} %wd_hbm.3), custom_call_target="tpu_custom_call" | custom-call | tf_op jit(solution)/shard_map/ffn_over/pallas_call | solution.py:307
  142.6 10.5 %all-to-all-start.1 = ((bf16[128,8,1024]{2,1,0:T(8,128)(2,1)}), bf16[128,8,1024]{2,1,0:T(8,128)(2,1)S(1)}, u32[]{:S(2)}, u32[]{:S(2)}) async-start(bf16[128,8,1024]{2,1,0:T(8,128)(2,1)} %bitcast.3), calls=%async_computation.1 | async-start | bytes 4194304 | tf_op jit(solution)/shard_map/all_to_all | solution.py:323
  153.2 25.0 %ffn_main.1 = bf16[1024,4096]{1,0:T(8,128)(2,1)} custom-call(bf16[128,40,1024]{2,1,0:T(8,128)(2,1)} %all_to_all.15.got_ref, bf16[1,4096,768]{2,1,0:T(8,128)(2,1)} %wg_hbm.1, bf16[1,4096,768]{2,1,0:T(8,128)(2,1)} %wu_hbm.1, bf16[1,768,4096]{2,1,0:T(8,128)(2,1)} %wd_hbm.3), custom_call_target="tpu_custom_call" | custom-call | tf_op jit(solution)/shard_map/ffn_main/pallas_call | solution.py:324
  178.2 0.6 all-to-all-done.1
  178.8 0.0 copy-start.2
  178.8 0.0 copy-start.3
  178.8 1.3 copy-done.2
  180.2 10.6 %all-to-all-start.2 = ((bf16[128,8,4096]{2,1,0:T(8,128)(2,1)}), bf16[128,8,4096]{2,1,0:T(8,128)(2,1)}, u32[]{:S(2)}, u32[]{:S(2)}) async-start(bf16[128,8,4096]{2,1,0:T(8,128)(2,1)} %bitcast.7), calls=%async_computation.2 | async-start | bytes 16777216 | tf_op jit(solution)/shard_map/all_to_all | solution.py:344
  190.8 0.0 copy-done.3
  190.8 0.7 copy.8.routes_ref
  191.5 0.0 copy-done.5
  191.5 0.7 copy.10.place_ref
  192.3 0.0 copy-done.4
  192.3 0.7 copy.9.gates_ref
  193.0 2.6 weights.1
  195.6 4.3 %combine_over.1.over_hbm = f32[128,4096]{1,0:T(8,128)} custom-call(bf16[256,256]{1,0:T(8,128)(2,1)} %get-tuple-element.8.cover_ref, bf16[1024,1024]{1,0:T(8,128)(2,1)} %bitcast.8), custom_call_target="tpu_custom_call" | custom-call | tf_op jit(solution)/shard_map/combine_over/pallas_call | solution.py:346
  199.9 95.7 %all-to-all-done.2 = bf16[128,8,4096]{2,1,0:T(8,128)(2,1)} async-done(((bf16[128,8,4096]{2,1,0:T(8,128)(2,1)}), bf16[128,8,4096]{2,1,0:T(8,128)(2,1)}, u32[]{:S(2)}, u32[]{:S(2)}) %all-to-all-start.2) | async-done | bytes 8388640 | tf_op jit(solution)/shard_map/all_to_all | solution.py:344
  295.6 6.1 %combine_main.1 = bf16[128,4096]{1,0:T(8,128)(2,1)} custom-call(bf16[256,1024]{1,0:T(8,128)(2,1)} %get-tuple-element.7.cmain_hbm, f32[128,4096]{1,0:T(8,128)} %combine_over.1.over_hbm, bf16[1024,4096]{1,0:T(8,128)(2,1)} %bitcast.6.main_ref), custom_call_target="tpu_custom_call" | custom-call | tf_op jit(solution)/shard_map/combine_main/pallas_call | solution.py:355
  (2 shorter events, 0.0 us)
Async XLA Ops:
  5.0 128.3 %copy-start = (bf16[1,4096,768]{2,1,0:T(8,128)(2,1)S(1)}, bf16[1,4096,768]{2,1,0:T(8,128)(2,1)}, u32[]{:S(2)}) copy-start(bf16[1,4096,768]{2,1,0:T(8,128)(2,1)} %wg_hbm.1) | copy-start | bytes 18874372
  5.0 128.2 %copy-start.1 = (bf16[1,4096,768]{2,1,0:T(8,128)(2,1)S(1)}, bf16[1,4096,768]{2,1,0:T(8,128)(2,1)}, u32[]{:S(2)}) copy-start(bf16[1,4096,768]{2,1,0:T(8,128)(2,1)} %wu_hbm.1) | copy-start | bytes 18874372
  142.6 36.2 %all-to-all-start.1 = ((bf16[128,8,1024]{2,1,0:T(8,128)(2,1)}), bf16[128,8,1024]{2,1,0:T(8,128)(2,1)S(1)}, u32[]{:S(2)}, u32[]{:S(2)}) async-start(bf16[128,8,1024]{2,1,0:T(8,128)(2,1)} %bitcast.3), calls=%async_computation.1 | async-start | bytes 4194304 | tf_op jit(solution)/shard_map/all_to_all | solution.py:323
  178.8 1.4 copy-start.2
  178.8 12.0 %copy-start.3 = (s32[128,8]{0,1:T(8,128)S(1)}, s32[128,8]{0,1:T(8,128)}, u32[]{:S(2)}) copy-start(s32[128,8]{0,1:T(8,128)} %param.8) | copy-start | bytes 12292
  178.8 12.7 %copy-start.5 = (s32[128]{0:T(128)S(1)}, s32[128]{0:T(128)}, u32[]{:S(2)}) copy-start(s32[128]{0:T(128)} %param.10) | copy-start | bytes 1540
  178.8 13.5 %copy-start.4 = (f32[128,8]{0,1:T(8,128)S(1)}, f32[128,8]{0,1:T(8,128)}, u32[]{:S(2)}) copy-start(f32[128,8]{0,1:T(8,128)} %param.9) | copy-start | bytes 12292
  180.2 115.4 %all-to-all-start.2 = ((bf16[128,8,4096]{2,1,0:T(8,128)(2,1)}), bf16[128,8,4096]{2,1,0:T(8,128)(2,1)}, u32[]{:S(2)}, u32[]{:S(2)}) async-start(bf16[128,8,4096]{2,1,0:T(8,128)(2,1)} %bitcast.7), calls=%async_computation.2 | async-start | bytes 16777216 | tf_op jit(solution)/shard_map/all_to_all | solution.py:344

commit v5 on v4

--- a/solution.py
+++ b/solution.py
@@ -6,6 +6,7 @@
 from jax.experimental import pallas as pl
 from jax.experimental.pallas import tpu as pltpu
 from jax.sharding import PartitionSpec as P
+
 
 AXES = ("node", "local")
 F32 = jnp.float32
@@ -41,6 +42,19 @@
     size = GROUP * 8
     grouped, plain = iota((size, size), 1 if back else 0), iota((size, size), 0 if back else 1)
     return (plain == grouped % GROUP * 8 + grouped // GROUP).astype(F32).astype(BF16)
+
+
+class Queue:
+    def __init__(self, copies, depth):
+        self.copies, self.depth, self.done = copies, depth, 0
+        for copy in copies[:depth]:
+            copy.start()
+
+    def next(self):
+        self.copies[self.done].wait()
+        self.done += 1
+        if self.done + self.depth <= len(self.copies):
+            self.copies[self.done + self.depth - 1].start()
 
 
 def pack_kernel(routes_ref, place_ref, tok_ref, out_ref, part_ref):
@@ -80,19 +94,6 @@
 
 def silu_mul(gate, up):
     return (gate / (1.0 + jnp.exp(-gate)) * up).astype(BF16)
-
-
-class Queue:
-    def __init__(self, copies, depth):
-        self.copies, self.depth, self.done = copies, depth, 0
-        for copy in copies[:depth]:
-            copy.start()
-
-    def next(self):
-        self.copies[self.done].wait()
-        self.done += 1
-        if self.done + self.depth <= len(self.copies):
-            self.copies[self.done + self.depth - 1].start()
 
 
 def ffn_main_kernel(
@@ -225,43 +226,29 @@
     place(cover_ref, lambda i: i // (2 * GROUP) * GROUP + i % GROUP, lambda i: 8 + i // GROUP % 2)
 
 
-def combine_over_kernel(cover_ref, over_ref, out_ref):
-    tok = out_ref.shape[0]
+def combine_kernel(cmain_ref, cover_ref, over_hbm, main_ref, out_ref, over_ref, early_ref, y_ref, over_sem, sems):
+    tok, _ = y_ref.shape
     wide = over_ref.shape[1]
     size = GROUP * 8
     pair = GROUP * 2
+    quarters = [slice(q * wide, (q + 1) * wide) for q in range(4)]
+    fetch = pltpu.make_async_copy(over_hbm, over_ref, over_sem)
+    fetch.start()
+    for q in range(2):
+        early_ref[q] = dot(cmain_ref[...], main_ref[:, quarters[q]])
+    fetch.wait()
     order = regroup(False)
-    parts = [
-        dot(order, over_ref[i : i + size, :]).astype(BF16) for i in range(0, over_ref.shape[0], size)
-    ]
-    for q in range(4):
+    parts = [dot(order, over_ref[i : i + size, :]).astype(BF16) for i in range(0, over_ref.shape[0], size)]
+    copies = []
+    for q, p in enumerate(quarters):
+        total = early_ref[q] if q < 2 else dot(cmain_ref[...], main_ref[:, p])
         over = jnp.concatenate([part[q * pair : (q + 1) * pair] for part in parts], axis=0)
-        total = dot(cover_ref[...], over)
-        out_ref[:, q * wide : (q + 1) * wide] = total[:tok] + total[tok:]
-
-
-COLUMNS = (1024, 1024, 1024, 512, 512)
-
-
-def combine_main_kernel(
-    cmain_hbm, over_hbm, main_ref, out_ref, cmain_ref, over_ref, x_ref, y_ref, in_sems, over_sems, out_sems, cmain_sem
-):
-    tok = y_ref.shape[0]
-    starts = [sum(COLUMNS[:i]) for i in range(len(COLUMNS))]
-    parts = [slice(a, a + n) for a, n in zip(starts, COLUMNS)]
-    coefs = pltpu.make_async_copy(cmain_hbm, cmain_ref, cmain_sem)
-    take = [pltpu.make_async_copy(main_ref.at[:, p], x_ref.at[:, p], in_sems.at[i]) for i, p in enumerate(parts)]
-    more = [pltpu.make_async_copy(over_hbm.at[:, p], over_ref.at[:, p], over_sems.at[i]) for i, p in enumerate(parts)]
-    give = [pltpu.make_async_copy(y_ref.at[:, p], out_ref.at[:, p], out_sems.at[i]) for i, p in enumerate(parts)]
-    queue = Queue([coefs] + [c for pair_of in zip(take, more) for c in pair_of], 5)
-    queue.next()
-    for i, p in enumerate(parts):
-        queue.next()
-        total = dot(cmain_ref[...], x_ref[:, p])
-        queue.next()
-        y_ref[:, p] = (total[:tok] + total[tok:] + over_ref[:, p]).astype(BF16)
-        give[i].start()
-    for copy in give:
+        total = total + dot(cover_ref[...], over)
+        y_ref[:, p] = (total[:tok] + total[tok:]).astype(BF16)
+        copy = pltpu.make_async_copy(y_ref.at[:, p], out_ref.at[:, p], sems.at[q])
+        copy.start()
+        copies.append(copy)
+    for copy in copies:
         copy.wait()
 
 
@@ -339,37 +326,25 @@
             pltpu.SemaphoreType.DMA((16,)),
             pltpu.SemaphoreType.DMA((4 * rows // 512,)),
         ],
-        compiler_params=params(0),
+        compiler_params=params(0, 63),
     )(got, w_gate, w_up, w_down)
     main = exchange(main.reshape(slots, 8, width)).reshape(rows, width)
 
-    total = pl.pallas_call(
-        combine_over_kernel,
-        name="combine_over",
-        grid=(1,),
-        in_specs=[whole(2 * tok, 2 * slots), whole(rows, wide)],
-        out_specs=whole(tok, width),
-        out_shape=shape((tok, width), F32),
-        compiler_params=params(1),
-    )(cover, over)
     return pl.pallas_call(
-        combine_main_kernel,
-        name="combine_main",
-        in_specs=[hbm] * 3,
+        combine_kernel,
+        name="combine",
+        in_specs=[vmem, vmem, hbm, vmem],
         out_specs=hbm,
         out_shape=shape((tok, width)),
         scratch_shapes=[
-            pltpu.VMEM((2 * tok, rows), BF16),
-            pltpu.VMEM((tok, width), F32),
-            pltpu.VMEM((rows, width), BF16),
+            pltpu.VMEM((rows, wide), BF16),
+            pltpu.VMEM((2, 2 * tok, wide), F32),
             pltpu.VMEM((tok, width), BF16),
-            pltpu.SemaphoreType.DMA((len(COLUMNS),)),
-            pltpu.SemaphoreType.DMA((len(COLUMNS),)),
-            pltpu.SemaphoreType.DMA((len(COLUMNS),)),
             pltpu.SemaphoreType.DMA,
+            pltpu.SemaphoreType.DMA((4,)),
         ],
-        compiler_params=params(0),
-    )(cmain, total, main)
+        compiler_params=params(0, 32),
+    )(cmain, cover, over, main)
 
 
 def solution(mesh):

time: 302 us -> 305 us (level)
  waiting for transfers between devices: 96.3 us -> 100 us
    all_to_all x1, waiting for transfers between devices: 95.7 us -> 100 us  [on_device(): main = exchange(main.reshape(slots, 8, width)).reshape(rows, width)]
    pallas_call x2 -> x1, Pallas kernels: 10.3 us -> 8.06 us  [on_device(): pl.pallas_call(combine_kernel, name='combine', in_specs=[vmem, vmem, hbm,...]
  transfers between devices with their start and end apart: 2 -> 2, of which waited for: 2 -> 2; matrix products, arithmetic and copies ran while one was open for 1% -> 1% of each run, Pallas kernels for 11% -> 9%
where the time goes in v5:
time: 305 us
  blocking collectives  128 us (42%)
  waiting for transfers between devices  100 us (33%)
  Pallas kernels  50 us (16%)
  starting transfers between devices  21.8 us (7%)
  local copies, waits for them, and re-layouts  4.13 us (1%)
    all_to_all x1, blocking collectives, on_device(): got = exchange(sent)  128 us
    all_to_all x1, waiting for transfers between devices, on_device(): main = exchange(main.reshape(slots, 8, width)).reshape(rows, width)  100 us
    pallas_call x1, Pallas kernels, on_device(): pl.pallas_call(ffn_main_kernel, name='ffn_main', in_specs=[hbm] * 4, out_...  25 us
    all_to_all x1, starting transfers between devices, on_device(): over = exchange(over.reshape(slots, 8, wide)).reshape(rows, wide)  11 us
    all_to_all x1, starting transfers between devices, on_device(): main = exchange(main.reshape(slots, 8, width)).reshape(rows, width)  10.8 us
    pallas_call x1, Pallas kernels, on_device(): pl.pallas_call(ffn_over_kernel, name='ffn_over', in_specs=[hbm, vmem, vme...  9.37 us
    pallas_call x1, Pallas kernels, on_device(): pl.pallas_call(combine_kernel, name='combine', in_specs=[vmem, vmem, hbm,...  8.06 us
  transfers between devices with their start and end apart: 2, of which 2 were waited for; matrix products, arithmetic and copies ran while one was open for 1% of the time, Pallas kernels for 9%

profile of v5, /device:TPU:103, one launch (start us, length us, event | category | flops | bytes accessed | tf_op | source)
XLA Modules:
  0.0 304.6 jit_solution(15765417440029961002)
XLA Ops:
  0.0 5.0 %pack.1 = bf16[128,40,1024]{2,1,0:T(8,128)(2,1)S(1)} custom-call(s32[8,128]{1,0:T(8,128)} %bitcast.8, s32[1,128]{1,0:T(1,128)} %bitcast.9, bf16[128,4096]{1,0:T(8,128)(2,1)} %tok_ref.1), custom_call_target="tpu_custom_call" | custom-call | tf_op jit(solution)/shard_map/pack/pallas_call | solution.py:274
  5.0 0.0 copy-start
  5.0 0.0 copy-start.1
  5.0 128.2 %all_to_all.15.got_ref = bf16[128,40,1024]{2,1,0:T(8,128)(2,1)} all-to-all(bf16[128,40,1024]{2,1,0:T(8,128)(2,1)S(1)} %pack.1), channel_id=1, replica_groups=mesh['node'=16,'local'=8] {'node','local'}, dimensions={0} | all-to-all | bytes 20971520 | tf_op jit(solution)/shard_map/all_to_all | solution.py:283
  133.2 0.0 copy-done
  133.2 0.0 copy-done.1
  133.2 9.4 %ffn_over.1 = bf16[1024,1024]{1,0:T(8,128)(2,1)} custom-call(bf16[128,40,1024]{2,1,0:T(8,128)(2,1)} %all_to_all.15.got_ref, bf16[1,4096,768]{2,1,0:T(8,128)(2,1)S(1)} %copy-done, bf16[1,4096,768]{2,1,0:T(8,128)(2,1)S(1)} %copy-done.1, bf16[1,768,4096]{2,1,0:T(8,128)(2,1)} %wd_hbm.3), custom_call_target="tpu_custom_call" | custom-call | tf_op jit(solution)/shard_map/ffn_over/pallas_call | solution.py:294
  142.6 11.0 %all-to-all-start.1 = ((bf16[128,8,1024]{2,1,0:T(8,128)(2,1)}), bf16[128,8,1024]{2,1,0:T(8,128)(2,1)}, u32[]{:S(2)}, u32[]{:S(2)}) async-start(bf16[128,8,1024]{2,1,0:T(8,128)(2,1)} %bitcast.3), calls=%async_computation.1 | async-start | bytes 4194304 | tf_op jit(solution)/shard_map/all_to_all | solution.py:310
  153.6 25.0 %ffn_main.1 = bf16[1024,4096]{1,0:T(8,128)(2,1)} custom-call(bf16[128,40,1024]{2,1,0:T(8,128)(2,1)} %all_to_all.15.got_ref, bf16[1,4096,768]{2,1,0:T(8,128)(2,1)} %wg_hbm.1, bf16[1,4096,768]{2,1,0:T(8,128)(2,1)} %wu_hbm.1, bf16[1,768,4096]{2,1,0:T(8,128)(2,1)} %wd_hbm.3), custom_call_target="tpu_custom_call" | custom-call | tf_op jit(solution)/shard_map/ffn_main/pallas_call | solution.py:311
  178.7 0.3 all-to-all-done.1
  178.9 0.0 copy-start.4
  178.9 0.0 copy-start.5
  178.9 10.8 %all-to-all-start.2 = ((bf16[128,8,4096]{2,1,0:T(8,128)(2,1)}), bf16[128,8,4096]{2,1,0:T(8,128)(2,1)}, u32[]{:S(2)}, u32[]{:S(2)}) async-start(bf16[128,8,4096]{2,1,0:T(8,128)(2,1)} %bitcast.7), calls=%async_computation.2 | async-start | bytes 16777216 | tf_op jit(solution)/shard_map/all_to_all | solution.py:331
  189.7 0.0 copy-done.4
  189.7 0.7 copy.8.routes_ref
  190.4 0.0 copy-done.5
  190.4 0.7 copy.9.gates_ref
  191.1 0.0 copy-done.6
  191.1 0.7 copy.10.place_ref
  191.9 2.6 weights.1
  194.4 100.0 %all-to-all-done.2 = bf16[128,8,4096]{2,1,0:T(8,128)(2,1)} async-done(((bf16[128,8,4096]{2,1,0:T(8,128)(2,1)}), bf16[128,8,4096]{2,1,0:T(8,128)(2,1)}, u32[]{:S(2)}, u32[]{:S(2)}) %all-to-all-start.2) | async-done | bytes 8388640 | tf_op jit(solution)/shard_map/all_to_all | solution.py:331
  294.4 1.0 copy-done.2
  295.5 0.9 copy-done.3
  296.4 8.1 %combine.1 = bf16[128,4096]{1,0:T(8,128)(2,1)} custom-call(bf16[256,1024]{1,0:T(8,128)(2,1)S(1)} %copy-done.2, bf16[256,256]{1,0:T(8,128)(2,1)S(1)} %copy-done.3, bf16[1024,1024]{1,0:T(8,128)(2,1)} %bitcast.4.over_hbm, bf16[1024,4096]{1,0:T(8,128)(2,1)} %bitcast.6.main_ref), custom_call_target="tpu_custom_call" | custom-call | tf_op jit(solution)/shard_map/combine/pallas_call | solution.py:333
  (3 shorter events, 0.0 us)
Async XLA Ops:
  5.0 128.3 %copy-start = (bf16[1,4096,768]{2,1,0:T(8,128)(2,1)S(1)}, bf16[1,4096,768]{2,1,0:T(8,128)(2,1)}, u32[]{:S(2)}) copy-start(bf16[1,4096,768]{2,1,0:T(8,128)(2,1)} %wg_hbm.1) | copy-start | bytes 18874372
  5.0 128.2 %copy-start.1 = (bf16[1,4096,768]{2,1,0:T(8,128)(2,1)S(1)}, bf16[1,4096,768]{2,1,0:T(8,128)(2,1)}, u32[]{:S(2)}) copy-start(bf16[1,4096,768]{2,1,0:T(8,128)(2,1)} %wu_hbm.1) | copy-start | bytes 18874372
  142.6 36.3 %all-to-all-start.1 = ((bf16[128,8,1024]{2,1,0:T(8,128)(2,1)}), bf16[128,8,1024]{2,1,0:T(8,128)(2,1)}, u32[]{:S(2)}, u32[]{:S(2)}) async-start(bf16[128,8,1024]{2,1,0:T(8,128)(2,1)} %bitcast.3), calls=%async_computation.1 | async-start | bytes 4194304 | tf_op jit(solution)/shard_map/all_to_all | solution.py:310
  178.9 10.8 %copy-start.4 = (s32[128,8]{0,1:T(8,128)S(1)}, s32[128,8]{0,1:T(8,128)}, u32[]{:S(2)}) copy-start(s32[128,8]{0,1:T(8,128)} %param.8) | copy-start | bytes 12292
  178.9 11.5 %copy-start.5 = (f32[128,8]{0,1:T(8,128)S(1)}, f32[128,8]{0,1:T(8,128)}, u32[]{:S(2)}) copy-start(f32[128,8]{0,1:T(8,128)} %param.9) | copy-start | bytes 12292
  178.9 12.2 %copy-start.6 = (s32[128]{0:T(128)S(1)}, s32[128]{0:T(128)}, u32[]{:S(2)}) copy-start(s32[128]{0:T(128)} %param.10) | copy-start | bytes 1540
  178.9 115.5 %all-to-all-start.2 = ((bf16[128,8,4096]{2,1,0:T(8,128)(2,1)}), bf16[128,8,4096]{2,1,0:T(8,128)(2,1)}, u32[]{:S(2)}, u32[]{:S(2)}) async-start(bf16[128,8,4096]{2,1,0:T(8,128)(2,1)} %bitcast.7), calls=%async_computation.2 | async-start | bytes 16777216 | tf_op jit(solution)/shard_map/all_to_all | solution.py:331
  294.4 1.0 copy-start.2
  295.5 0.9 copy-start.3

commit v6 on v5

--- a/solution.py
+++ b/solution.py
@@ -155,7 +155,7 @@
 
 
 def ffn_over_kernel(
-    got_ref, wg_ref, wu_ref, wd_hbm, out_ref, x_ref, wd_ref, part_ref, back_ref, in_sems, out_sems
+    got_ref, wg_ref, wu_ref, wd_ref, out_ref, x_ref, part_ref, back_ref, in_sems, out_sems
 ):
     groups = part_ref.shape[0]
     wide = x_ref.shape[2]
@@ -166,10 +166,7 @@
     lines = [slice(g * size, (g + 1) * size) for g in range(groups)]
     take = [pltpu.make_async_copy(got_ref.at[s, 32:40, :], x_ref.at[s], in_sems.at[g]) for g, s in enumerate(slots)]
     give = [pltpu.make_async_copy(back_ref.at[r, :], out_ref.at[r, :], out_sems.at[g]) for g, r in enumerate(lines)]
-    downs = [
-        pltpu.make_async_copy(wd_hbm.at[0, :, p], wd_ref.at[:, p], in_sems.at[groups + q]) for q, p in enumerate(quarters)
-    ]
-    queue = Queue(take + downs, 5)
+    queue = Queue(take, 4)
     order = regroup(False)
     for g in range(groups):
         queue.next()
@@ -182,8 +179,7 @@
         gate, up = (one, two) if q == 0 else (gate + one, up + two)
     hidden = silu_mul(gate, up)
     for q, p in enumerate(quarters):
-        queue.next()
-        out = dot(hidden, wd_ref[:, p]).astype(BF16)
+        out = dot(hidden, wd_ref[0, :, p]).astype(BF16)
         for g in range(groups):
             part_ref[g, q * pair : (q + 1) * pair, :] = out[g * pair : (g + 1) * pair]
     order = regroup(True)
@@ -294,18 +290,17 @@
     over = pl.pallas_call(
         ffn_over_kernel,
         name="ffn_over",
-        in_specs=[hbm, vmem, vmem, hbm],
+        in_specs=[hbm, vmem, vmem, vmem],
         out_specs=hbm,
         out_shape=shape((rows, wide)),
         scratch_shapes=[
             pltpu.VMEM((slots, 8, wide), BF16),
-            pltpu.VMEM((hid, width), BF16),
             pltpu.VMEM((slots // GROUP, 8 * GROUP, wide), BF16),
             pltpu.VMEM((rows, wide), BF16),
-            pltpu.SemaphoreType.DMA((slots // GROUP + 4,)),
+            pltpu.SemaphoreType.DMA((slots // GROUP,)),
             pltpu.SemaphoreType.DMA((slots // GROUP,)),
         ],
-        compiler_params=params(0, 36),
+        compiler_params=params(0, 20),
     )(got, w_gate, w_up, w_down)
     over = exchange(over.reshape(slots, 8, wide)).reshape(rows, wide)
     main = pl.pallas_call(

time: 305 us -> 303 us (level)
  no operation moved by 1% of the time
where the time goes in v6:
time: 303 us
  blocking collectives  128 us (42%)
  waiting for transfers between devices  100 us (33%)
  Pallas kernels  48.4 us (16%)
  starting transfers between devices  21.7 us (7%)
  local copies, waits for them, and re-layouts  4.15 us (1%)
    all_to_all x1, blocking collectives, on_device(): got = exchange(sent)  128 us
    all_to_all x1, waiting for transfers between devices, on_device(): main = exchange(main.reshape(slots, 8, width)).reshape(rows, width)  100 us
    pallas_call x1, Pallas kernels, on_device(): pl.pallas_call(ffn_main_kernel, name='ffn_main', in_specs=[hbm] * 4, out_...  24.9 us
    all_to_all x1, starting transfers between devices, on_device(): over = exchange(over.reshape(slots, 8, wide)).reshape(rows, wide)  11 us
    all_to_all x1, starting transfers between devices, on_device(): main = exchange(main.reshape(slots, 8, width)).reshape(rows, width)  10.8 us
    pallas_call x1, Pallas kernels, on_device(): pl.pallas_call(combine_kernel, name='combine', in_specs=[vmem, vmem, hbm,...  8.06 us
    pallas_call x1, Pallas kernels, on_device(): pl.pallas_call(ffn_over_kernel, name='ffn_over', in_specs=[hbm, vmem, vme...  7.82 us
  transfers between devices with their start and end apart: 2, of which 2 were waited for; matrix products, arithmetic and copies ran while one was open for 1% of the time, Pallas kernels for 9%

profile of v6, /device:TPU:103, one launch (start us, length us, event | category | flops | bytes accessed | tf_op | source)
XLA Modules:
  0.0 303.0 jit_solution(15172103974593798063)
XLA Ops:
  0.0 5.0 %pack.1 = bf16[128,40,1024]{2,1,0:T(8,128)(2,1)S(1)} custom-call(s32[8,128]{1,0:T(8,128)} %bitcast.8, s32[1,128]{1,0:T(1,128)} %bitcast.9, bf16[128,4096]{1,0:T(8,128)(2,1)} %tok_ref.1), custom_call_target="tpu_custom_call" | custom-call | tf_op jit(solution)/shard_map/pack/pallas_call | solution.py:270
  5.0 0.0 copy-start.1
  5.0 0.0 copy-start.2
  5.0 0.0 copy-start.3
  5.0 128.1 %all_to_all.15.got_ref = bf16[128,40,1024]{2,1,0:T(8,128)(2,1)S(1)} all-to-all(bf16[128,40,1024]{2,1,0:T(8,128)(2,1)S(1)} %pack.1), channel_id=1, replica_groups=mesh['node'=16,'local'=8] {'node','local'}, dimensions={0} | all-to-all | bytes 20971520 | tf_op jit(solution)/shard_map/all_to_all | solution.py:279
  133.1 0.0 copy-done.1
  133.1 0.0 copy-done.2
  133.1 0.0 copy-done.3
  133.1 0.0 copy-start
  133.2 7.8 %ffn_over.1 = bf16[1024,1024]{1,0:T(8,128)(2,1)} custom-call(bf16[128,40,1024]{2,1,0:T(8,128)(2,1)S(1)} %all_to_all.15.got_ref, bf16[1,4096,768]{2,1,0:T(8,128)(2,1)S(1)} %copy-done.1, bf16[1,4096,768]{2,1,0:T(8,128)(2,1)S(1)} %copy-done.2, bf16[1,768,4096]{2,1,0:T(8,128)(2,1)S(1)} %copy-done.3), custom_call_target="tpu_custom_call" | custom-call | tf_op jit(solution)/shard_map/ffn_over/pallas_call | solution.py:290
  141.0 0.0 copy-done
  141.0 11.0 %all-to-all-start.1 = ((bf16[128,8,1024]{2,1,0:T(8,128)(2,1)}), bf16[128,8,1024]{2,1,0:T(8,128)(2,1)}, u32[]{:S(2)}, u32[]{:S(2)}) async-start(bf16[128,8,1024]{2,1,0:T(8,128)(2,1)} %bitcast.3), calls=%async_computation.1 | async-start | bytes 4194304 | tf_op jit(solution)/shard_map/all_to_all | solution.py:305
  152.0 24.9 %ffn_main.1 = bf16[1024,4096]{1,0:T(8,128)(2,1)} custom-call(bf16[128,40,1024]{2,1,0:T(8,128)(2,1)} %copy-done, bf16[1,4096,768]{2,1,0:T(8,128)(2,1)} %wg_hbm.1, bf16[1,4096,768]{2,1,0:T(8,128)(2,1)} %wu_hbm.1, bf16[1,768,4096]{2,1,0:T(8,128)(2,1)} %wd_hbm.1), custom_call_target="tpu_custom_call" | custom-call | tf_op jit(solution)/shard_map/ffn_main/pallas_call | solution.py:306
  176.9 0.4 all-to-all-done.1
  177.3 10.8 %all-to-all-start.2 = ((bf16[128,8,4096]{2,1,0:T(8,128)(2,1)}), bf16[128,8,4096]{2,1,0:T(8,128)(2,1)}, u32[]{:S(2)}, u32[]{:S(2)}) async-start(bf16[128,8,4096]{2,1,0:T(8,128)(2,1)} %bitcast.7), calls=%async_computation.2 | async-start | bytes 16777216 | tf_op jit(solution)/shard_map/all_to_all | solution.py:326
  188.0 0.0 copy-done.6
  188.0 0.7 copy.8.routes_ref
  188.8 0.7 copy.9.gates_ref
  189.5 0.7 copy.10.place_ref
  190.2 2.6 weights.1
  192.8 100.0 %all-to-all-done.2 = bf16[128,8,4096]{2,1,0:T(8,128)(2,1)} async-done(((bf16[128,8,4096]{2,1,0:T(8,128)(2,1)}), bf16[128,8,4096]{2,1,0:T(8,128)(2,1)}, u32[]{:S(2)}, u32[]{:S(2)}) %all-to-all-start.2) | async-done | bytes 8388640 | tf_op jit(solution)/shard_map/all_to_all | solution.py:326
  292.8 1.0 copy-done.4
  293.8 0.9 copy-done.5
  294.7 8.1 %combine.1 = bf16[128,4096]{1,0:T(8,128)(2,1)} custom-call(bf16[256,1024]{1,0:T(8,128)(2,1)S(1)} %copy-done.4, bf16[256,256]{1,0:T(8,128)(2,1)S(1)} %copy-done.5, bf16[1024,1024]{1,0:T(8,128)(2,1)} %bitcast.4.over_hbm, bf16[1024,4096]{1,0:T(8,128)(2,1)} %bitcast.6.main_ref), custom_call_target="tpu_custom_call" | custom-call | tf_op jit(solution)/shard_map/combine/pallas_call | solution.py:328
  (7 shorter events, 0.0 us)
Async XLA Ops:
  5.0 128.2 %copy-start.1 = (bf16[1,4096,768]{2,1,0:T(8,128)(2,1)S(1)}, bf16[1,4096,768]{2,1,0:T(8,128)(2,1)}, u32[]{:S(2)}) copy-start(bf16[1,4096,768]{2,1,0:T(8,128)(2,1)} %wg_hbm.1) | copy-start | bytes 18874372
  5.0 128.2 %copy-start.2 = (bf16[1,4096,768]{2,1,0:T(8,128)(2,1)S(1)}, bf16[1,4096,768]{2,1,0:T(8,128)(2,1)}, u32[]{:S(2)}) copy-start(bf16[1,4096,768]{2,1,0:T(8,128)(2,1)} %wu_hbm.1) | copy-start | bytes 18874372
  5.0 128.1 %copy-start.3 = (bf16[1,768,4096]{2,1,0:T(8,128)(2,1)S(1)}, bf16[1,768,4096]{2,1,0:T(8,128)(2,1)}, u32[]{:S(2)}) copy-start(bf16[1,768,4096]{2,1,0:T(8,128)(2,1)} %wd_hbm.1) | copy-start | bytes 18874372
  133.1 7.8 %copy-start = (bf16[128,40,1024]{2,1,0:T(8,128)(2,1)}, bf16[128,40,1024]{2,1,0:T(8,128)(2,1)S(1)}, u32[]{:S(2)}) copy-start(bf16[128,40,1024]{2,1,0:T(8,128)(2,1)S(1)} %all_to_all.15.got_ref) | copy-start | bytes 31457284
  141.0 36.3 %all-to-all-start.1 = ((bf16[128,8,1024]{2,1,0:T(8,128)(2,1)}), bf16[128,8,1024]{2,1,0:T(8,128)(2,1)}, u32[]{:S(2)}, u32[]{:S(2)}) async-start(bf16[128,8,1024]{2,1,0:T(8,128)(2,1)} %bitcast.3), calls=%async_computation.1 | async-start | bytes 4194304 | tf_op jit(solution)/shard_map/all_to_all | solution.py:305
  177.2 10.8 %copy-start.6 = (s32[128,8]{0,1:T(8,128)S(1)}, s32[128,8]{0,1:T(8,128)}, u32[]{:S(2)}) copy-start(s32[128,8]{0,1:T(8,128)} %param.8) | copy-start | bytes 12292
  177.2 11.5 %copy-start.7 = (f32[128,8]{0,1:T(8,128)S(1)}, f32[128,8]{0,1:T(8,128)}, u32[]{:S(2)}) copy-start(f32[128,8]{0,1:T(8,128)} %param.9) | copy-start | bytes 12292
  177.2 12.2 %copy-start.8 = (s32[128]{0:T(128)S(1)}, s32[128]{0:T(128)}, u32[]{:S(2)}) copy-start(s32[128]{0:T(128)} %param.10) | copy-start | bytes 1540
  177.3 115.5 %all-to-all-start.2 = ((bf16[128,8,4096]{2,1,0:T(8,128)(2,1)}), bf16[128,8,4096]{2,1,0:T(8,128)(2,1)}, u32[]{:S(2)}, u32[]{:S(2)}) async-start(bf16[128,8,4096]{2,1,0:T(8,128)(2,1)} %bitcast.7), calls=%async_computation.2 | async-start | bytes 16777216 | tf_op jit(solution)/shard_map/all_to_all | solution.py:326
  292.8 1.0 copy-start.4
  293.8 0.9 copy-start.5
